TPU v7x, 512 devices: a whole 4x8x8 slice. The times are simulated.
512 devices in a mesh: grp: 8 (over y), ctx: 64 (over z, x, core).
Axes of the slice: x: 4, y: 8, z: 8, core: 2. Of those that a mesh axis runs over, the one named last changes fastest.
Arguments:
- tokens: bfloat16 [65536, 2048], P(('grp', 'ctx')), parts along dimension 0, may hold values from -32 to 32
- gain_in: float32 [2048], replicated, may hold values from 0.1 to 1.9
- long_filter: bfloat16 [2048, 8192], P('ctx'), may hold values from -0.0625 to 0.0625
- skip_gain: float32 [2048], P('ctx'), may hold values from 0.5 to 1.5
- gain_ffn: float32 [2048], replicated, may hold values from 0.1 to 1.9
- router: bfloat16 [2048, 16], replicated, may hold values from -1 to 1
- w_up: bfloat16 [2048, 16384], P(None, 'ctx'), may hold values from -0.125 to 0.125
- w_down: bfloat16 [16384, 2048], P('ctx'), may hold values from -0.375 to 0.375
- expert_id: int32 [65536], P(('grp', 'ctx')), parts along dimension 0, may hold values from 0 to 15
- slot_index: int32 [65536], P(('grp', 'ctx')), parts along dimension 0, may hold values from 0 to 15, as said below
Outputs:
- layer_out: bfloat16 [65536, 2048], P(('grp', 'ctx')), parts along dimension 0
There are 8 independent parts, one for each index of `grp`. A program takes and returns all parts, laid end to end along the dimension named above; an argument that names none is the same for every part. Nothing has to cross between parts.
Inputs may be any that keep to these rules, and one draw needn't show every extreme that they name: Among the 128 tokens of one device no two share both expert_id and slot_index; one expert, the same for all devices, receives 4 * 4 tokens from every device; the others receive at most as many.
All inputs are finite; a program needn't handle non-finite values.
Results may differ from a plain program's by a relative error of at most 0.0085.
Values may be sent and summed in bfloat16 or wider, within the bound.
A program may use at most 64 MiB of HBM per device.

v0:
```python
import math

import jax
import jax.numpy as jnp
from jax import lax
from jax.sharding import PartitionSpec as P


def swapped(array, axis, stride):
    return lax.ppermute(array, axis, [(i, i ^ 1 << stride) for i in range(lax.axis_size(axis))])


def rms_scale(values, gain):
    floats = values.astype(jnp.float32)
    return floats * lax.rsqrt(jnp.mean(floats * floats, axis=1, keepdims=True) + 1e-06) * gain


def angle_table(first, second, period):
    product = first[:, None] * second[None, :] % period
    angles = product.astype(jnp.float32) * (2.0 * math.pi / period)
    return (jnp.cos(angles), jnp.sin(angles))


def matmul_high(left, right):
    return jnp.dot(left, right, precision=lax.Precision.HIGH, preferred_element_type=jnp.float32)


def long_conv(spread, long_filter, skip_gain, groups, tok_rows):
    channels = spread.shape[0]
    half_chan = channels // 2
    size_two = 2 * groups * tok_rows
    stacked = (
        jnp.concatenate([spread, long_filter], axis=0)
        .astype(jnp.float32)
        .reshape(2 * channels, groups, tok_rows)
    )
    block_idx = jnp.arange(groups, dtype=jnp.int32)
    freq_outer = jnp.arange(2 * groups, dtype=jnp.int32)
    row_idx = jnp.arange(tok_rows, dtype=jnp.int32)
    cos_outer, sin_outer = angle_table(block_idx, freq_outer, 2 * groups)
    cos_twist, sin_twist = angle_table(freq_outer, row_idx, size_two)
    cos_inner, sin_inner = angle_table(row_idx, row_idx, tok_rows)
    outer_fwd = jnp.concatenate([cos_outer, -sin_outer], axis=1)
    first = jnp.einsum("cpn,pk->ckn", stacked, outer_fwd, precision=lax.Precision.HIGH)
    first_re = first[:, : 2 * groups]
    first_im = first[:, 2 * groups :]
    twisted = jnp.concatenate(
        [first_re * cos_twist + first_im * sin_twist, first_im * cos_twist - first_re * sin_twist],
        axis=2,
    )
    inner_fwd = jnp.concatenate(
        [
            jnp.concatenate([cos_inner, -sin_inner], axis=1),
            jnp.concatenate([sin_inner, cos_inner], axis=1),
        ],
        axis=0,
    )
    spec = matmul_high(twisted.reshape(-1, 2 * tok_rows), inner_fwd).reshape(
        2 * channels, 2 * groups, 2 * tok_rows
    )
    sig_re, sig_im = (spec[:channels, :, :tok_rows], spec[:channels, :, tok_rows:])
    filt_re, filt_im = (spec[channels:, :, :tok_rows], spec[channels:, :, tok_rows:])
    prod_re = sig_re * filt_re - sig_im * filt_im
    prod_im = sig_re * filt_im + sig_im * filt_re
    packed = jnp.concatenate(
        [prod_re[:half_chan] - prod_im[half_chan:], prod_im[:half_chan] + prod_re[half_chan:]],
        axis=2,
    )
    inner_inv = jnp.concatenate(
        [
            jnp.concatenate([cos_inner, sin_inner], axis=1),
            jnp.concatenate([-sin_inner, cos_inner], axis=1),
        ],
        axis=0,
    )
    back = matmul_high(packed.reshape(-1, 2 * tok_rows), inner_inv).reshape(
        half_chan, 2 * groups, 2 * tok_rows
    )
    back_re, back_im = (back[:, :, :tok_rows], back[:, :, tok_rows:])
    turned = jnp.stack(
        [back_re * cos_twist - back_im * sin_twist, back_im * cos_twist + back_re * sin_twist],
        axis=1,
    )
    outer_inv = jnp.stack(
        [jnp.stack([cos_outer, sin_outer], axis=0), jnp.stack([-sin_outer, cos_outer], axis=0)],
        axis=0,
    )
    result = jnp.einsum("cskn,sopk->ocpn", turned, outer_inv, precision=lax.Precision.HIGH)
    result = result.reshape(channels, groups * tok_rows) / size_two
    return result + skip_gain[:, None] * spread.astype(jnp.float32)


def body(
    tokens, gain_in, long_filter, skip_gain, gain_ffn, router, w_up, w_down, expert_id, slot_index
):
    tok_rows, feat_dim = tokens.shape
    groups = lax.axis_size("ctx")
    normed = rms_scale(tokens, gain_in).astype(jnp.bfloat16)
    spread = lax.all_to_all(normed.T, "ctx", split_axis=0, concat_axis=1, tiled=True)
    convolved = long_conv(spread, long_filter, skip_gain, groups, tok_rows).astype(jnp.bfloat16)
    returned_conv = lax.all_to_all(convolved, "ctx", split_axis=1, concat_axis=0, tiled=True)
    middle = (tokens.astype(jnp.float32) + returned_conv.T.astype(jnp.float32)).astype(jnp.bfloat16)
    ffn_in = rms_scale(middle, gain_ffn).astype(jnp.bfloat16)
    logits = jnp.dot(ffn_in, router, preferred_element_type=jnp.float32)
    chosen = lax.broadcasted_iota(jnp.int32, logits.shape, 1) == expert_id[:, None]
    gate_value = jax.nn.sigmoid(jnp.sum(jnp.where(chosen, logits, 0.0), axis=1))
    slots_dev = 2 * tok_rows // groups
    target = expert_id * (4 * slots_dev) + slot_index
    onehot_send = (
        lax.broadcasted_iota(jnp.int32, (groups * slots_dev, tok_rows), 0) == target[None, :]
    ).astype(jnp.bfloat16)
    onehot_back = (
        lax.broadcasted_iota(jnp.int32, (tok_rows, groups * slots_dev), 1) == target[:, None]
    ).astype(jnp.bfloat16)
    outgoing = jnp.dot(onehot_send, ffn_in, preferred_element_type=jnp.float32).astype(jnp.bfloat16)
    received = lax.all_to_all(
        outgoing.reshape(groups, slots_dev, feat_dim),
        "ctx",
        split_axis=0,
        concat_axis=0,
        tiled=True,
    )
    own_rows = received.reshape(groups * slots_dev, feat_dim)
    current = own_rows
    for bit_pos in (0, 1):
        partner = swapped(current, "ctx", bit_pos)
        current = jnp.concatenate([current, partner], axis=0)
    hidden = jax.nn.gelu(
        jnp.dot(current, w_up, preferred_element_type=jnp.float32), approximate=False
    ).astype(jnp.bfloat16)
    partial_sum = jnp.dot(hidden, w_down, preferred_element_type=jnp.float32)
    for bit_pos in (1, 0):
        halves = partial_sum.reshape(2, -1, feat_dim)
        partial_sum = halves[0] + swapped(halves[1].astype(jnp.bfloat16), "ctx", bit_pos).astype(
            jnp.float32
        )
    expert_rows = partial_sum.astype(jnp.bfloat16)
    arrived = lax.all_to_all(
        expert_rows.reshape(groups, slots_dev, feat_dim),
        "ctx",
        split_axis=0,
        concat_axis=0,
        tiled=True,
    )
    expert_out = jnp.dot(
        onehot_back,
        arrived.reshape(groups * slots_dev, feat_dim),
        preferred_element_type=jnp.float32,
    )
    layer_out = (middle.astype(jnp.float32) + gate_value[:, None] * expert_out).astype(jnp.bfloat16)
    return layer_out


def solution(mesh):
    return jax.shard_map(
        body,
        mesh=mesh,
        in_specs=(
            P(("grp", "ctx"), None),
            P(),
            P("ctx", None),
            P("ctx"),
            P(),
            P(),
            P(None, "ctx"),
            P("ctx", None),
            P(("grp", "ctx")),
            P(("grp", "ctx")),
        ),
        out_specs=P(("grp", "ctx"), None),
        check_vma=False,
    )
```

profile of v0, /device:TPU:6, one launch (start us, length us, event | category | flops | bytes accessed | tf_op | source)
XLA Modules:
  0.0 280.6 jit_solution(14466702236119282367)
XLA Ops:
  0.0 0.0 copy-start
  0.0 1.3 fusion.27
  1.3 1.2 fusion.53
  2.6 1.0 copy.26
  3.6 13.8 %all-to-all-start = ((bf16[64,32,128]{2,1,0:T(8,128)(2,1)}), bf16[64,32,128]{2,1,0:T(8,128)(2,1)S(1)}, u32[]{:S(2)}, u32[]{:S(2)}) async-start(bf16[64,32,128]{2,1,0:T(8,128)(2,1)} %bitcast.1), calls=%async_computation | async-start | bytes 1048576 | tf_op jit(solution)/shard_map/all_to_all | solution.py:99
  17.4 1.2 copy.37
  18.6 0.3 fusion.121
  18.8 0.1 copy.28
  18.9 0.1 copy.29
  19.0 0.1 fusion.133
  19.2 0.1 sine_negate_fusion
  19.3 0.3 fusion.129
  19.6 0.1 fusion.131
  19.8 0.3 fusion.119
  20.1 14.9 %all-to-all-done = bf16[64,32,128]{2,1,0:T(8,128)(2,1)S(1)} async-done(((bf16[64,32,128]{2,1,0:T(8,128)(2,1)}), bf16[64,32,128]{2,1,0:T(8,128)(2,1)S(1)}, u32[]{:S(2)}, u32[]{:S(2)}) %all-to-all-start) | async-done | bytes 524320 | tf_op jit(solution)/shard_map/all_to_all | solution.py:99
  35.0 0.2 copy.49
  35.2 2.4 convolution_bitcast_fusion
  37.6 1.3 multiply_add_fusion
  38.8 7.0 %fusion = f32[64,128,256]{2,1,0:T(8,128)S(1)} fusion(f32[64,128,128]{1,2,0:T(8,128)S(1)} %get-tuple-element.8, f32[64,128,128]{1,2,0:T(8,128)S(1)} %get-tuple-element.7, f32[128,128]{1,0:T(8,128)S(1)} %get-tuple-element.20, f32[128,128]{1,0:T(8,128)S(1)} %get-tuple-element.19, f32[128,128]{1,0:T(8,128)S(1)} %fusion.129), kind=kOutput, calls=%fused_computation | convolution fusion | flops 3223519232 | bytes 16973824 | tf_op jit(solution)/shard_map/dot_general | solution.py:25
  45.9 0.7 multiply_add_fusion.1
  46.5 0.4 slice_subtract_fusion
  47.0 1.0 fusion.13
  48.0 0.0 copy-start.4
  48.0 0.3 subtract_bitcast_fusion
  48.3 0.0 copy-start.6
  48.3 0.0 copy-start.7
  48.3 0.8 fusion.23
  49.1 0.0 copy-done.4
  49.2 0.0 copy-start.1
  49.2 0.3 fusion.40
  49.5 0.0 copy-start.3
  49.5 1.1 copy.32
  50.6 5.9 %all-to-all-start.1 = ((bf16[32,64,128]{2,0,1:T(8,128)(2,1)}), bf16[32,64,128]{2,0,1:T(8,128)(2,1)S(1)}, u32[]{:S(2)}, u32[]{:S(2)}) async-start(bf16[32,64,128]{2,0,1:T(8,128)(2,1)} %copy.32), calls=%async_computation.1 | async-start | bytes 1048576 | tf_op jit(solution)/shard_map/all_to_all | solution.py:101
  56.5 17.5 %all-to-all-done.1 = bf16[32,64,128]{2,0,1:T(8,128)(2,1)S(1)} async-done(((bf16[32,64,128]{2,0,1:T(8,128)(2,1)}), bf16[32,64,128]{2,0,1:T(8,128)(2,1)S(1)}, u32[]{:S(2)}, u32[]{:S(2)}) %all-to-all-start.1) | async-done | bytes 524320 | tf_op jit(solution)/shard_map/all_to_all | solution.py:101
  74.1 1.1 convert_element_type.152
  75.2 1.6 copy.33
  76.8 0.2 fusion.31
  77.0 1.5 convolution_convert_fusion
  78.5 1.5 reshape.193
  80.0 34.6 %all_to_all.36 = bf16[64,4,2048]{2,1,0:T(4,128)(2,1)} all-to-all(bf16[64,4,2048]{2,1,0:T(4,128)(2,1)S(1)} %reshape.193), channel_id=1, replica_groups=mesh['grp'=8,'ctx'=64] {'ctx'}, dimensions={0} | all-to-all | bytes 2097152 | tf_op jit(solution)/shard_map/all_to_all | solution.py:116
  114.6 1.3 reshape.194
  115.9 1.9 collective-permute-start
  117.8 2.6 collective-permute-done
  120.5 0.2 pad_maximum_fusion.1
  120.6 3.0 %collective-permute-start.1 = (bf16[512,2048]{1,0:T(8,128)(2,1)S(1)}, bf16[512,2048]{1,0:T(8,128)(2,1)}, u32[]{:S(2)}, u32[]{:S(2)}) collective-permute-start(bf16[512,2048]{1,0:T(8,128)(2,1)S(1)} %pad_maximum_fusion.1), channel_id=1, source_target_pairs={{0,2},{1,3},{2,0},{3,1},{4,6},{5,7},{6,4},{7,5},{8,10},{9,11},{10,... | collective-permute-start | bytes 6291464 | tf_op jit(solution)/shard_map/ppermute | solution.py:10
  123.6 0.0 copy-done.2
  123.6 46.7 %collective-permute-done.1 = bf16[512,2048]{1,0:T(8,128)(2,1)} collective-permute-done((bf16[512,2048]{1,0:T(8,128)(2,1)S(1)}, bf16[512,2048]{1,0:T(8,128)(2,1)}, u32[]{:S(2)}, u32[]{:S(2)}) %collective-permute-start.1) | collective-permute-done | bytes 2097184 | tf_op jit(solution)/shard_map/ppermute | solution.py:10
  170.3 11.8 %fusion.51 = f32[1024,2048]{1,0:T(8,128)} fusion(bf16[256,2048]{1,0:T(8,128)(2,1)S(1)} %copy-done, bf16[2048,256]{1,0:T(8,128)(2,1)} %param.16, bf16[512,2048]{1,0:T(8,128)(2,1)} %collective-permute-done.1, bf16[256,2048]{1,0:T(8,128)(2,1)} %copy-done.2, bf16[256,2048]{1,0:T(8,128)(2,1)S(1)} %reshape.194), kind=kOutput, calls=%fused_computation.77 | convolution fusion | flops 2177105920 | bytes 14680064 | tf_op jit(solution)/shard_map/dot_general | solution.py:131
  182.1 2.5 slice.112
  184.6 2.8 collective-permute-start.2
  187.4 46.0 %collective-permute-done.2 = bf16[512,2048]{1,0:T(8,128)(2,1)S(1)} collective-permute-done((bf16[512,2048]{1,0:T(8,128)(2,1)S(1)}, bf16[512,2048]{1,0:T(8,128)(2,1)S(1)}, u32[]{:S(2)}, u32[]{:S(2)}) %collective-permute-start.2) | collective-permute-done | bytes 2097184 | tf_op jit(solution)/shard_map/ppermute | solution.py:10
  233.4 2.8 %slice_add_fusion = f32[512,2048]{1,0:T(8,128)S(1)} fusion(f32[1024,2048]{1,0:T(8,128)} %fusion.51, bf16[512,2048]{1,0:T(8,128)(2,1)S(1)} %collective-permute-done.2), kind=kLoop, calls=%fused_computation.5 | loop fusion | flops 2097152 | bytes 10485760 | tf_op jit(solution)/shard_map/add | solution.py:134
  236.2 0.1 slice.113
  236.4 0.0 copy-start.5
  236.4 2.1 collective-permute-start.3
  238.4 2.6 collective-permute-done.3
  241.1 0.3 fusion.12
  241.4 1.2 reshape.195
  242.6 5.7 %all-to-all-start.3 = ((bf16[64,4,2048]{2,1,0:T(4,128)(2,1)}), bf16[64,4,2048]{2,1,0:T(4,128)(2,1)S(1)}, u32[]{:S(2)}, u32[]{:S(2)}) async-start(bf16[64,4,2048]{2,1,0:T(4,128)(2,1)} %reshape.195), calls=%async_computation.3 | async-start | bytes 2097152 | tf_op jit(solution)/shard_map/all_to_all | solution.py:138
  248.3 0.0 copy-done.5
  248.3 0.3 fusion.26
  248.6 28.5 %all-to-all-done.3 = bf16[64,4,2048]{2,1,0:T(4,128)(2,1)S(1)} async-done(((bf16[64,4,2048]{2,1,0:T(4,128)(2,1)}), bf16[64,4,2048]{2,1,0:T(4,128)(2,1)S(1)}, u32[]{:S(2)}, u32[]{:S(2)}) %all-to-all-start.3) | async-done | bytes 1048608 | tf_op jit(solution)/shard_map/all_to_all | solution.py:138
  277.1 1.1 reshape.196
  278.2 2.4 fusion.11
  (11 shorter events, 0.1 us)
Async XLA Ops:
  0.0 170.3 %copy-start = (bf16[256,2048]{1,0:T(8,128)(2,1)S(1)}, bf16[256,2048]{1,0:T(8,128)(2,1)}, u32[]{:S(2)}) copy-start(bf16[256,2048]{1,0:T(8,128)(2,1)} %param.17) | copy-start | bytes 3145732
  3.6 31.4 %all-to-all-start = ((bf16[64,32,128]{2,1,0:T(8,128)(2,1)}), bf16[64,32,128]{2,1,0:T(8,128)(2,1)S(1)}, u32[]{:S(2)}, u32[]{:S(2)}) async-start(bf16[64,32,128]{2,1,0:T(8,128)(2,1)} %bitcast.1), calls=%async_computation | async-start | bytes 1048576 | tf_op jit(solution)/shard_map/all_to_all | solution.py:99
  48.0 1.2 copy-start.4
  48.3 8.2 %copy-start.6 = (s32[128]{0:T(128)S(1)}, s32[128]{0:T(128)}, u32[]{:S(2)}) copy-start(s32[128]{0:T(128)} %param.19) | copy-start | bytes 1540
  48.3 8.2 %copy-start.7 = (s32[128]{0:T(128)S(1)}, s32[128]{0:T(128)}, u32[]{:S(2)}) copy-start(s32[128]{0:T(128)} %param.18) | copy-start | bytes 1540
  49.2 27.6 %copy-start.1 = (bf16[128,2048]{1,0:T(8,128)(2,1)S(1)}, bf16[128,2048]{1,0:T(8,128)(2,1)}, u32[]{:S(2)}) copy-start(bf16[128,2048]{1,0:T(8,128)(2,1)} %param.10) | copy-start | bytes 1572868
  49.5 27.5 %copy-start.3 = (f32[2048]{0:T(1024)S(1)}, f32[2048]{0:T(1024)}, u32[]{:S(2)}) copy-start(f32[2048]{0:T(1024)} %param.14) | copy-start | bytes 24580
  50.6 23.4 %all-to-all-start.1 = ((bf16[32,64,128]{2,0,1:T(8,128)(2,1)}), bf16[32,64,128]{2,0,1:T(8,128)(2,1)S(1)}, u32[]{:S(2)}, u32[]{:S(2)}) async-start(bf16[32,64,128]{2,0,1:T(8,128)(2,1)} %copy.32), calls=%async_computation.1 | async-start | bytes 1048576 | tf_op jit(solution)/shard_map/all_to_all | solution.py:101
  115.9 4.6 %collective-permute-start = (bf16[256,2048]{1,0:T(8,128)(2,1)S(1)}, bf16[256,2048]{1,0:T(8,128)(2,1)S(1)}, u32[]{:S(2)}, u32[]{:S(2)}) collective-permute-start(bf16[256,2048]{1,0:T(8,128)(2,1)S(1)} %reshape.194), channel_id=1, source_target_pairs={{0,1},{1,0},{2,3},{3,2},{4,5},{5,4},{6,7},{7,6},{8,9},{9,8},{10,11... | collective-permute-start | bytes 3145736 | tf_op jit(solution)/shard_map/ppermute | solution.py:10
  120.5 3.2 %copy-start.2 = (bf16[256,2048]{1,0:T(8,128)(2,1)}, bf16[256,2048]{1,0:T(8,128)(2,1)S(1)}, u32[]{:S(2)}) copy-start(bf16[256,2048]{1,0:T(8,128)(2,1)S(1)} %collective-permute-done) | copy-start | bytes 3145732
  120.6 49.7 %collective-permute-start.1 = (bf16[512,2048]{1,0:T(8,128)(2,1)S(1)}, bf16[512,2048]{1,0:T(8,128)(2,1)}, u32[]{:S(2)}, u32[]{:S(2)}) collective-permute-start(bf16[512,2048]{1,0:T(8,128)(2,1)S(1)} %pad_maximum_fusion.1), channel_id=1, source_target_pairs={{0,2},{1,3},{2,0},{3,1},{4,6},{5,7},{6,4},{7,5},{8,10},{9,11},{10,... | collective-permute-start | bytes 6291464 | tf_op jit(solution)/shard_map/ppermute | solution.py:10
  184.6 48.7 %collective-permute-start.2 = (bf16[512,2048]{1,0:T(8,128)(2,1)S(1)}, bf16[512,2048]{1,0:T(8,128)(2,1)S(1)}, u32[]{:S(2)}, u32[]{:S(2)}) collective-permute-start(bf16[512,2048]{1,0:T(8,128)(2,1)S(1)} %slice.112), channel_id=1, source_target_pairs={{0,2},{1,3},{2,0},{3,1},{4,6},{5,7},{6,4},{7,5},{8,10},{9,11},{10,... | collective-permute-start | bytes 6291464 | tf_op jit(solution)/shard_map/ppermute | solution.py:10
  236.4 11.9 %copy-start.5 = (bf16[2048,16]{0,1:T(8,128)(2,1)S(1)}, bf16[2048,16]{0,1:T(8,128)(2,1)}, u32[]{:S(2)}) copy-start(bf16[2048,16]{0,1:T(8,128)(2,1)} %param.15) | copy-start | bytes 196612
  236.4 4.7 %collective-permute-start.3 = (bf16[256,2048]{1,0:T(8,128)(2,1)S(1)}, bf16[256,2048]{1,0:T(8,128)(2,1)S(1)}, u32[]{:S(2)}, u32[]{:S(2)}) collective-permute-start(bf16[256,2048]{1,0:T(8,128)(2,1)S(1)} %slice.113), channel_id=1, source_target_pairs={{0,1},{1,0},{2,3},{3,2},{4,5},{5,4},{6,7},{7,6},{8,9},{9,8},{10,11... | collective-permute-start | bytes 3145736 | tf_op jit(solution)/shard_map/ppermute | solution.py:10
  242.6 34.5 %all-to-all-start.3 = ((bf16[64,4,2048]{2,1,0:T(4,128)(2,1)}), bf16[64,4,2048]{2,1,0:T(4,128)(2,1)S(1)}, u32[]{:S(2)}, u32[]{:S(2)}) async-start(bf16[64,4,2048]{2,1,0:T(4,128)(2,1)} %reshape.195), calls=%async_computation.3 | async-start | bytes 2097152 | tf_op jit(solution)/shard_map/all_to_all | solution.py:138
where the time goes:
time: 282 us; the launch traced here: 281 us
  waiting for transfers between devices  159 us (56%)
  starting transfers between devices  35 us (12%)
  blocking collectives  34.6 us (12%)
  matrix products  27.2 us (10%)
  local copies, waits for them, and re-layouts  13 us (5%)
  other arithmetic  11.5 us (4%)
    ppermute x4, waiting for transfers between devices, swapped(): lax.ppermute(array, axis, [(i, i ^ 1 << stride) for i in range(lax.axis_s...  97.9 us
    all_to_all x1, blocking collectives, body(): lax.all_to_all(outgoing.reshape(groups, slots_dev, feat_dim), 'ctx', spli...  34.6 us
    all_to_all x1, waiting for transfers between devices, body(): lax.all_to_all(expert_rows.reshape(groups, slots_dev, feat_dim), 'ctx', s...  28.5 us
    all_to_all x1, waiting for transfers between devices, body(): lax.all_to_all(convolved, 'ctx', split_axis=1, concat_axis=0, tiled=True)  17.5 us
    all_to_all x1, waiting for transfers between devices, body(): lax.all_to_all(normed.T, 'ctx', split_axis=0, concat_axis=1, tiled=True)  14.9 us
    all_to_all x1, starting transfers between devices, body(): lax.all_to_all(normed.T, 'ctx', split_axis=0, concat_axis=1, tiled=True)  13.8 us
    dot_general x1, matrix products, body(): partial_sum = jnp.dot(hidden, w_down, preferred_element_type=jnp.float32)  11.8 us
    ppermute x4, starting transfers between devices, swapped(): lax.ppermute(array, axis, [(i, i ^ 1 << stride) for i in range(lax.axis_s...  9.7 us
  transfers between devices with their start and end apart: 7, of which 7 were waited for; matrix products, arithmetic and copies ran while one was open for 1% of the time, Pallas kernels for 0%

commit v1 on v0

v1 whole, which is shorter than its diff:
```python
import functools
import math

import jax
import jax.numpy as jnp
from jax import lax
from jax.experimental import pallas as pl
from jax.experimental.pallas import tpu as pltpu
from jax.sharding import PartitionSpec as P

MESH = pl.DeviceIdType.MESH


def angle_table(first, second, period):
    product = first[:, None] * second[None, :] % period
    angles = product.astype(jnp.float32) * (2.0 * math.pi / period)
    return (jnp.cos(angles), jnp.sin(angles))


def enter(peers, me, n):
    barrier = pltpu.get_barrier_semaphore()

    def greet(i, carry):
        pl.semaphore_signal(
            barrier, inc=1, device_id={"ctx": lax.rem(me + i, n)}, device_id_type=MESH
        )
        return carry

    lax.fori_loop(1, n, greet, 0)
    pl.semaphore_wait(barrier, n - 1)


def class_of(dev):
    z, x, core = dev // 8, dev // 2 % 4, dev % 2
    parity = (x + x // 2) % 2
    return parity * 2 + core, z * 2 + x // 2


def owner_class(dev):
    x, core = dev // 2 % 4, dev % 2
    return (x + x // 2) % 2 * 2 + core


def source_of(dev, rank):
    x, core = dev // 2 % 4, dev % 2
    parity = (x + x // 2) % 2
    src_x = parity + rank % 2 * (3 - 2 * parity)
    return (rank // 2 * 4 + src_x) * 2 + core


def spread_kernel(n, toks, aux, toks_out, aux_out, local, s_tok, r_tok, s_aux, r_aux):
    me = lax.axis_index("ctx")
    enter(None, me, n)
    group, rank = class_of(me)
    place = group * 16 + rank

    def tok_copy(peer, slot):
        return pltpu.make_async_remote_copy(
            toks.at[peer], toks_out.at[place], s_tok.at[peer], r_tok.at[slot],
            device_id={"ctx": peer}, device_id_type=MESH)

    def aux_copy(peer, slot):
        return pltpu.make_async_remote_copy(
            aux, aux_out.at[place], s_aux.at[peer], r_aux.at[slot],
            device_id={"ctx": peer}, device_id_type=MESH)

    def send(i, carry):
        peer = lax.rem(me + i, n)
        aux_copy(peer, me).start()
        tok_copy(peer, me).start()
        return carry

    lax.fori_loop(1, n, send, 0)
    own = [
        pltpu.make_async_copy(toks.at[me], toks_out.at[place], local.at[0]),
        pltpu.make_async_copy(aux, aux_out.at[place], local.at[1]),
    ]
    for copy in own:
        copy.start()
    for copy in own:
        copy.wait()

    def finish(i, carry):
        peer = lax.rem(me + i, n)
        aux_copy(peer, peer).wait()
        tok_copy(peer, peer).wait()
        return carry

    lax.fori_loop(1, n, finish, 0)


def spread(toks, aux, n):
    return pl.pallas_call(
        functools.partial(spread_kernel, n),
        out_shape=(
            jax.ShapeDtypeStruct(toks.shape, toks.dtype),
            jax.ShapeDtypeStruct((n,) + aux.shape, aux.dtype),
        ),
        in_specs=[pl.BlockSpec(memory_space=pl.ANY)] * 2,
        out_specs=[pl.BlockSpec(memory_space=pl.ANY)] * 2,
        scratch_shapes=[
            pltpu.SemaphoreType.DMA((2,)),
            pltpu.SemaphoreType.DMA((n,)),
            pltpu.SemaphoreType.DMA((n,)),
            pltpu.SemaphoreType.DMA((n,)),
            pltpu.SemaphoreType.DMA((n,)),
        ],
        compiler_params=pltpu.CompilerParams(collective_id=0, has_side_effects=True),
    )(toks, aux)


def dispatch_kernel(n, rows, rows_out, local, s_sem, r_sem):
    me = lax.axis_index("ctx")
    enter(None, me, n)

    def row_copy(peer, slot):
        return pltpu.make_async_remote_copy(
            rows.at[owner_class(peer), peer // 4], rows_out.at[me], s_sem.at[peer], r_sem.at[slot],
            device_id={"ctx": peer}, device_id_type=MESH)

    def send(i, carry):
        row_copy(lax.rem(me + i, n), me).start()
        return carry

    lax.fori_loop(1, n, send, 0)
    own = pltpu.make_async_copy(rows.at[owner_class(me), me // 4], rows_out.at[me], local)
    own.start()
    own.wait()

    def finish(i, carry):
        peer = lax.rem(me + i, n)
        row_copy(peer, peer).wait()
        return carry

    lax.fori_loop(1, n, finish, 0)


def dispatch(rows, n):
    return pl.pallas_call(
        functools.partial(dispatch_kernel, n),
        out_shape=jax.ShapeDtypeStruct((n,) + rows.shape[2:], rows.dtype),
        in_specs=[pl.BlockSpec(memory_space=pl.ANY)],
        out_specs=pl.BlockSpec(memory_space=pl.ANY),
        scratch_shapes=[
            pltpu.SemaphoreType.DMA,
            pltpu.SemaphoreType.DMA((n,)),
            pltpu.SemaphoreType.DMA((n,)),
        ],
        compiler_params=pltpu.CompilerParams(collective_id=1, has_side_effects=True),
    )(rows)


def combine_kernel(n, rows, rows_out, local, s_sem, r_sem):
    me = lax.axis_index("ctx")
    enter(None, me, n)
    expert = me // 4
    group, my_rank = class_of(me)
    core, parity = me % 2, group // 2

    def holder(other):
        pair = other % 2
        return (other // 2 * 4 + 2 * pair + (parity + pair) % 2) * 2 + core

    def row_copy(rank, slot):
        return pltpu.make_async_remote_copy(
            rows.at[rank], rows_out.at[expert], s_sem.at[rank], r_sem.at[slot],
            device_id={"ctx": source_of(me, rank)}, device_id_type=MESH)

    def send(rank, carry):
        @pl.when(source_of(me, rank) != me)
        def _():
            row_copy(rank, expert).start()
        return carry

    lax.fori_loop(0, 16, send, 0)

    @pl.when(source_of(me, my_rank) == me)
    def _():
        own = pltpu.make_async_copy(rows.at[my_rank], rows_out.at[expert], local)
        own.start()
        own.wait()

    def finish(i, carry):
        @pl.when(source_of(me, i) != me)
        def _():
            row_copy(i, i).wait_send()

        @pl.when(holder(i) != me)
        def _():
            row_copy(0, i).wait_recv()
        return carry

    lax.fori_loop(0, 16, finish, 0)


def combine(rows, n):
    return pl.pallas_call(
        functools.partial(combine_kernel, n),
        out_shape=jax.ShapeDtypeStruct(rows.shape, rows.dtype),
        in_specs=[pl.BlockSpec(memory_space=pl.ANY)],
        out_specs=pl.BlockSpec(memory_space=pl.ANY),
        scratch_shapes=[
            pltpu.SemaphoreType.DMA,
            pltpu.SemaphoreType.DMA((16,)),
            pltpu.SemaphoreType.DMA((16,)),
        ],
        compiler_params=pltpu.CompilerParams(collective_id=2, has_side_effects=True),
    )(rows)


def tables(order):
    quarter = 4 * jnp.arange(64, dtype=jnp.int32) + 1
    lane = jnp.arange(128, dtype=jnp.int32)
    cos_outer, sin_outer = angle_table(order, quarter, 256)
    cos_twist, sin_twist = angle_table(quarter, lane, 32768)
    cos_inner, sin_inner = angle_table(lane, lane, 128)
    return cos_outer, sin_outer, cos_twist, sin_twist, cos_inner, sin_inner


def dot_high(left, right):
    return jnp.dot(left, right, precision=lax.Precision.HIGH, preferred_element_type=jnp.float32)


def forward(blocks, spec, order):
    cos_outer, sin_outer, cos_twist, sin_twist, cos_inner, sin_inner = tables(order)
    outer = jnp.concatenate([cos_outer, -sin_outer], axis=1)
    first = jnp.einsum(spec, blocks, outer, precision=lax.Precision.HIGH)
    re, im = first[:, :64], first[:, 64:]
    twisted = jnp.concatenate(
        [re * cos_twist + im * sin_twist, im * cos_twist - re * sin_twist], axis=2)
    inner = jnp.concatenate(
        [
            jnp.concatenate([cos_inner, -sin_inner], axis=1),
            jnp.concatenate([sin_inner, cos_inner], axis=1),
        ],
        axis=0,
    )
    return dot_high(twisted.reshape(-1, 256), inner).reshape(-1, 64, 256)


def inverse(prod, order):
    cos_outer, sin_outer, cos_twist, sin_twist, cos_inner, sin_inner = tables(order)
    inner = jnp.concatenate(
        [
            jnp.concatenate([cos_inner, sin_inner], axis=1),
            jnp.concatenate([-sin_inner, cos_inner], axis=1),
        ],
        axis=0,
    )
    back = dot_high(prod.reshape(-1, 256), inner).reshape(-1, 64, 256)
    re, im = back[:, :, :128], back[:, :, 128:]
    turned = jnp.concatenate(
        [re * cos_twist - im * sin_twist, im * cos_twist + re * sin_twist], axis=1)
    outer = jnp.concatenate([cos_outer, -sin_outer], axis=1) / 8192.0
    return jnp.einsum("ckn,pk->cpn", turned, outer, precision=lax.Precision.HIGH)


def swapped(array, bit):
    return lax.ppermute(array, "ctx", [(i, i ^ (1 << bit)) for i in range(64)])


def body(
    tokens, gain_in, long_filter, skip_gain, gain_ffn, router, w_up, w_down, expert_id, slot_index
):
    n = lax.axis_size("ctx")
    me = lax.axis_index("ctx")
    far_up, far_down = swapped(w_up, 1), swapped(w_down, 1)
    ups = [w_up, swapped(w_up, 0), far_up, swapped(far_up, 0)]
    downs = [w_down, swapped(w_down, 0), far_down, swapped(far_down, 0)]

    floats = tokens.astype(jnp.float32)
    scale = lax.rsqrt(jnp.mean(floats * floats, axis=1) + 1e-06)
    target = expert_id * 16 + slot_index
    aux = jnp.stack([scale, target.astype(jnp.float32)], axis=0)
    toks, auxes = spread(tokens.T.reshape(n, 32, 128), aux, n)

    place = jnp.arange(64, dtype=jnp.int32)
    parity, core, rank = place // 32, place // 16 % 2, place % 16
    order = (rank // 2 * 4 + parity + rank % 2 * (3 - 2 * parity)) * 2 + core

    gain = lax.dynamic_slice(gain_in, (me * 32,), (32,))
    tok_f = toks.astype(jnp.float32)
    normed = (tok_f * auxes[:, 0][:, None, :] * gain[None, :, None]).astype(jnp.bfloat16)
    normed = normed.astype(jnp.float32)
    spec_f = forward(
        long_filter.astype(jnp.float32).reshape(32, 64, 128), "cpn,pk->ckn",
        jnp.arange(64, dtype=jnp.int32))
    spec_x = forward(normed, "pcn,pk->ckn", order)
    x_re, x_im = spec_x[:, :, :128], spec_x[:, :, 128:]
    f_re, f_im = spec_f[:, :, :128], spec_f[:, :, 128:]
    prod = jnp.concatenate([x_re * f_re - x_im * f_im, x_re * f_im + x_im * f_re], axis=2)
    conv = inverse(prod, order)
    conv_out = (conv.transpose(1, 0, 2) + skip_gain[None, :, None] * normed).astype(jnp.bfloat16)
    middle = (tok_f + conv_out.astype(jnp.float32)).astype(jnp.bfloat16)

    chosen = auxes[:, 1].astype(jnp.int32)
    onehot = (
        lax.broadcasted_iota(jnp.int32, (64, 256, 128), 1) == chosen[:, None, :]
    ).astype(jnp.bfloat16)
    packed = jnp.einsum("pst,pct->psc", onehot, middle, preferred_element_type=jnp.float32)
    packed = packed.astype(jnp.bfloat16).reshape(4, 4, 4, 16, 16, 32)
    packed = packed.transpose(0, 3, 1, 4, 2, 5).reshape(4, 16, 64, 128)
    received = dispatch(packed, n)
    mid_rows = received.reshape(64, 4, 16, 4, 32).transpose(1, 3, 2, 0, 4).reshape(256, 2048)

    rows_f = mid_rows.astype(jnp.float32)
    row_scale = lax.rsqrt(jnp.mean(rows_f * rows_f, axis=1, keepdims=True) + 1e-06)
    ffn_in = (rows_f * row_scale * gain_ffn).astype(jnp.bfloat16)
    logits = jnp.dot(ffn_in, router, preferred_element_type=jnp.float32)
    mine = lax.broadcasted_iota(jnp.int32, logits.shape, 1) == me // 4
    gate_value = jax.nn.sigmoid(jnp.sum(jnp.where(mine, logits, 0.0), axis=1, keepdims=True))
    total = jnp.zeros((256, 2048), jnp.float32)
    for up, down in zip(ups, downs):
        hidden = jax.nn.gelu(
            jnp.dot(ffn_in, up, preferred_element_type=jnp.float32), approximate=False
        ).astype(jnp.bfloat16)
        total = total + jnp.dot(hidden, down, preferred_element_type=jnp.float32)
    expert_out = total.astype(jnp.bfloat16).astype(jnp.float32)
    out_rows = (rows_f + gate_value * expert_out).astype(jnp.bfloat16)
    arrived = combine(out_rows.reshape(16, 16, 2048), n)
    pick = (
        lax.broadcasted_iota(jnp.int32, (128, 256), 1) == target[:, None]
    ).astype(jnp.bfloat16)
    return jnp.dot(
        pick, arrived.reshape(256, 2048), preferred_element_type=jnp.float32
    ).astype(jnp.bfloat16)


def solution(mesh):
    return jax.shard_map(
        body,
        mesh=mesh,
        in_specs=(
            P(("grp", "ctx"), None),
            P(),
            P("ctx", None),
            P("ctx"),
            P(),
            P(),
            P(None, "ctx"),
            P("ctx", None),
            P(("grp", "ctx")),
            P(("grp", "ctx")),
        ),
        out_specs=P(("grp", "ctx"), None),
        check_vma=False,
    )
```

time: 282 us -> 213 us (0.76)
  the two profiles are of different devices: /device:TPU:6 before, /device:TPU:142 now
where the time goes in v1:
time: 213 us; the launch traced here: 212 us
  Pallas kernels  119 us (56%)
  local copies, waits for them, and re-layouts  39.7 us (19%)
  matrix products  31 us (15%)
  starting transfers between devices  14.3 us (7%)
  other arithmetic  8.04 us (4%)
    pallas_call x1, Pallas kernels, spread(): pl.pallas_call(functools.partial(spread_kernel, n), out_shape=(jax.ShapeD...  45.5 us
    pallas_call x1, Pallas kernels, dispatch(): pl.pallas_call(functools.partial(dispatch_kernel, n), out_shape=jax.Shape...  40.6 us
    pallas_call x1, Pallas kernels, combine(): pl.pallas_call(functools.partial(combine_kernel, n), out_shape=jax.ShapeD...  32.5 us
    dot_general x4, matrix products, body(): total = total + jnp.dot(hidden, down, preferred_element_type=jnp.float32)  20.5 us
    convert_element_type x3, local copies, waits for them, and re-layouts, body(): rows_f = mid_rows.astype(jnp.float32)  17.6 us
    ppermute x6, starting transfers between devices, swapped(): return lax.ppermute(array, 'ctx', [(i, i ^ 1 << bit) for i in range(64)])  14.3 us
    transpose x1, local copies, waits for them, and re-layouts, body(): packed = packed.transpose(0, 3, 1, 4, 2, 5).reshape(4, 16, 64, 128)  9.53 us
    reshape x1, local copies, waits for them, and re-layouts, body(): packed = packed.transpose(0, 3, 1, 4, 2, 5).reshape(4, 16, 64, 128)  6.06 us
  transfers between devices with their start and end apart: 6, of which 0 were waited for; matrix products, arithmetic and copies ran while one was open for 34% of the time, Pallas kernels for 41%

profile of v1, /device:TPU:142, one launch (start us, length us, event | category | flops | bytes accessed | tf_op | source)
XLA Modules:
  0.0 211.9 jit_solution(6306728360025136746)
XLA Ops:
  0.0 0.0 copy-start
  0.0 2.0 collective-permute-start
  2.1 2.7 %collective-permute-start.2 = (bf16[2048,256]{1,0:T(8,128)(2,1)}, bf16[2048,256]{1,0:T(8,128)(2,1)}, u32[]{:S(2)}, u32[]{:S(2)}) collective-permute-start(bf16[2048,256]{1,0:T(8,128)(2,1)} %param.16), channel_id=1, source_target_pairs={{0,2},{1,3},{2,0},{3,1},{4,6},{5,7},{6,4},{7,5},{8,10},{9,11},{10,... | collective-permute-start | bytes 3145736 | tf_op jit(solution)/shard_map/ppermute | solution.py:259
  4.8 2.1 %collective-permute-start.1 = (bf16[256,2048]{1,0:T(8,128)(2,1)}, bf16[256,2048]{1,0:T(8,128)(2,1)}, u32[]{:S(2)}, u32[]{:S(2)}) collective-permute-start(bf16[256,2048]{1,0:T(8,128)(2,1)} %param.17), channel_id=1, source_target_pairs={{0,1},{1,0},{2,3},{3,2},{4,5},{5,4},{6,7},{7,6},{8,9},{9,8},{10,11... | collective-permute-start | bytes 3145736 | tf_op jit(solution)/shard_map/ppermute | solution.py:259
  6.9 3.1 %collective-permute-start.3 = (bf16[256,2048]{1,0:T(8,128)(2,1)}, bf16[256,2048]{1,0:T(8,128)(2,1)}, u32[]{:S(2)}, u32[]{:S(2)}) collective-permute-start(bf16[256,2048]{1,0:T(8,128)(2,1)} %param.17), channel_id=1, source_target_pairs={{0,2},{1,3},{2,0},{3,1},{4,6},{5,7},{6,4},{7,5},{8,10},{9,11},{10,... | collective-permute-start | bytes 3145736 | tf_op jit(solution)/shard_map/ppermute | solution.py:259
  10.1 0.3 fusion.228
  10.4 0.3 fusion.235
  10.6 1.2 multiply_reduce_fusion.1
  11.9 2.0 copy.28
  13.9 0.7 convert_bitcast_fusion
  14.6 0.6 pad_maximum_fusion.8.aux
  15.2 45.5 %shard_map.100 = (bf16[64,32,128]{2,1,0:T(8,128)(2,1)}, f32[64,2,128]{2,1,0:T(2,128)}) custom-call(bf16[64,32,128]{2,1,0:T(8,128)(2,1)} %bitcast.61, f32[2,128]{1,0:T(2,128)} %pad_maximum_fusion.8.aux), custom_call_target="tpu_custom_call" | custom-call | tf_op jit(solution)/shard_map/pallas_call | solution.py:93
  60.6 1.0 fusion.373
  61.6 0.2 fusion.237
  61.8 0.3 fusion.240
  62.1 0.0 copy-done.2
  62.2 0.1 copy.37
  62.3 0.8 dynamic_slice.3
  63.0 1.3 fusion.26
  64.3 0.8 convolution_bitcast_fusion.1
  65.1 0.8 convolution_bitcast_fusion
  66.0 1.0 multiply_add_fusion.3
  66.9 1.0 fusion.7
  68.0 1.0 fusion.11
  69.0 0.3 multiply_subtract_fusion.1
  69.3 1.0 fusion.15
  70.3 0.3 multiply_subtract_fusion
  70.6 0.0 copy-start.3
  70.6 0.0 copy-start.5
  70.7 0.8 fusion.19
  71.5 0.2 copy-done.3
  71.7 0.0 copy-done.5
  71.7 2.2 %fusion.23 = bf16[64,256,32]{1,2,0:T(8,128)(2,1)S(1)} fusion(s32[64,128]{1,0:T(8,128)S(1)} %bitcast.68, bf16[64,32,128]{2,1,0:T(8,128)(2,1)S(1)} %copy-done.3, f32[64,32,128]{2,0,1:T(8,128)S(1)} %fusion.19, f32[32]{0:T(128)S(1)} %copy-done.5, f32[32]{0:T(128)S(1)} %dynamic_slice.3, f32[64,128]{1,0:T(8,128)S(1)} %bitcast.66), kind=kOutput, calls=%fused_computation.32 | convolution fusion | flops 139722752 | bytes 2687232 | tf_op jit(solution)/shard_map/pst,pct->psc/dot_general | solution.py:300
  73.9 3.1 %copy.31 = bf16[64,256,32]{2,1,0:T(8,128)(2,1)} copy(bf16[64,256,32]{1,2,0:T(8,128)(2,1)S(1)} %fusion.23) | data formatting | bytes 2097152 | tf_op jit(solution)/shard_map/convert_element_type | solution.py:301
  77.1 9.5 %copy.32 = bf16[4,16,4,16,4,32]{5,4,3,2,1,0:T(4,128)(2,1)} copy(bf16[4,16,4,16,4,32]{5,3,1,4,2,0:T(8,128)(2,1)} %bitcast.58) | data formatting | bytes 2097152 | tf_op jit(solution)/shard_map/transpose | solution.py:302
  86.6 6.1 %reshape.225.rows = bf16[4,16,64,128]{3,2,1,0:T(8,128)(2,1)} reshape(bf16[4,16,4,16,4,32]{5,4,3,2,1,0:T(4,128)(2,1)} %copy.32) | data formatting | bytes 2097152 | tf_op jit(solution)/shard_map/reshape | solution.py:302
  92.6 40.6 %shard_map.101 = bf16[64,64,128]{2,1,0:T(8,128)(2,1)} custom-call(bf16[4,16,64,128]{3,2,1,0:T(8,128)(2,1)} %reshape.225.rows), custom_call_target="tpu_custom_call" | custom-call | tf_op jit(solution)/shard_map/pallas_call | solution.py:139
  133.2 0.0 copy-start.1
  133.2 3.9 %copy.33 = f32[64,64,128]{0,2,1:T(8,128)} copy(bf16[64,64,128]{2,1,0:T(8,128)(2,1)} %shard_map.101) | data formatting | bytes 3145728 | tf_op jit(solution)/shard_map/convert_element_type | solution.py:306
  137.2 0.0 copy-done.1
  137.2 0.2 multiply_reduce_fusion
  137.4 6.9 %copy.34 = f32[4,4,16,64,32]{4,3,2,1,0:T(8,128)} copy(f32[4,4,16,64,32]{3,4,1,2,0:T(8,128)} %bitcast.57) | data formatting | bytes 4194304 | tf_op jit(solution)/shard_map/convert_element_type | solution.py:306
  144.3 6.7 %reshape.228 = f32[256,2048]{1,0:T(8,128)S(1)} reshape(f32[4,4,16,64,32]{4,3,2,1,0:T(8,128)} %copy.34) | data formatting | bytes 4194304 | tf_op jit(solution)/shard_map/convert_element_type | solution.py:306
  151.0 0.1 reduce_sum.36
  151.1 0.1 reduce_sum.37
  151.3 0.1 copy.38
  151.4 0.1 rsqrt.27
  151.5 0.0 copy-done.4
  151.5 0.2 multiply_convert_fusion
  151.8 0.4 fusion.24
  152.2 4.7 %fusion.84 = f32[256,2048]{1,0:T(8,128)} fusion(bf16[256,2048]{1,0:T(8,128)(2,1)} %param.17, bf16[256,2048]{1,0:T(8,128)(2,1)S(1)} %multiply_convert_fusion, bf16[2048,256]{1,0:T(8,128)(2,1)} %param.16), kind=kOutput, calls=%fused_computation.139 | convolution fusion | flops 541130752 | bytes 5242880 | tf_op jit(solution)/shard_map/dot_general | solution.py:317
  156.9 0.0 collective-permute-done.2
  156.9 2.1 collective-permute-start.4
  158.9 0.0 collective-permute-done.3
  159.0 2.3 %collective-permute-start.5 = (bf16[256,2048]{1,0:T(8,128)(2,1)}, bf16[256,2048]{1,0:T(8,128)(2,1)}, u32[]{:S(2)}, u32[]{:S(2)}) collective-permute-start(bf16[256,2048]{1,0:T(8,128)(2,1)} %collective-permute-done.3), channel_id=1, source_target_pairs={{0,1},{1,0},{2,3},{3,2},{4,5},{5,4},{6,7},{7,6},{8,9},{9,8},{10,11... | collective-permute-start | bytes 3145736 | tf_op jit(solution)/shard_map/ppermute | solution.py:259
  161.2 0.0 collective-permute-done
  161.3 0.0 collective-permute-done.1
  161.3 5.4 %convolution_add_fusion.2 = f32[256,2048]{1,0:T(8,128)} fusion(f32[256,2048]{1,0:T(8,128)} %fusion.84, bf16[256,2048]{1,0:T(8,128)(2,1)} %collective-permute-done.1, bf16[256,2048]{1,0:T(8,128)(2,1)S(1)} %multiply_convert_fusion, bf16[2048,256]{1,0:T(8,128)(2,1)} %collective-permute-done), kind=kOutput, calls=%fused_computation.5 | convolution fusion | flops 541655040 | bytes 7340032 | tf_op jit(solution)/shard_map/dot_general | solution.py:317
  166.6 5.4 %convolution_add_fusion.1 = f32[256,2048]{1,0:T(8,128)} fusion(f32[256,2048]{1,0:T(8,128)} %convolution_add_fusion.2, bf16[256,2048]{1,0:T(8,128)(2,1)} %collective-permute-done.3, bf16[256,2048]{1,0:T(8,128)(2,1)S(1)} %multiply_convert_fusion, bf16[2048,256]{1,0:T(8,128)(2,1)} %collective-permute-done.2), kind=kOutput, calls=%fused_computation.4 | convolution fusion | flops 541655040 | bytes 7340032 | tf_op jit(solution)/shard_map/dot_general | solution.py:317
  172.0 0.0 collective-permute-done.4
  172.0 0.0 collective-permute-done.5
  172.0 5.0 %fusion.6 = bf16[256,2048]{1,0:T(8,128)(2,1)} fusion(f32[256,2048]{1,0:T(8,128)S(1)} %reshape.228, f32[256,2048]{1,0:T(8,128)} %convolution_add_fusion.1, bf16[256,2048]{1,0:T(8,128)(2,1)} %collective-permute-done.5, f32[256]{0:T(256)S(1)} %add_divide_fusion, bf16[256,2048]{1,0:T(8,128)(2,1)S(1)} %multiply_convert_fusion, ...), kind=kOutput, calls=%fused_computation.10 | convolution fusion | flops 544276480 | bytes 8389632 | tf_op jit(solution)/shard_map/dot_general | solution.py:317
  177.0 32.5 %shard_map.102 = bf16[16,16,2048]{2,1,0:T(8,128)(2,1)} custom-call(bf16[16,16,2048]{2,1,0:T(8,128)(2,1)} %bitcast.63), custom_call_target="tpu_custom_call" | custom-call | tf_op jit(solution)/shard_map/pallas_call | solution.py:197
  209.6 2.4 %convolution_convert_fusion = bf16[128,2048]{1,0:T(8,128)(2,1)} fusion(bf16[256,2048]{1,0:T(8,128)(2,1)} %bitcast.59, s32[128]{0:T(128)S(1)} %get-tuple-element.10), kind=kOutput, calls=%fused_computation.11 | convolution fusion | flops 134512640 | bytes 1573376 | tf_op jit(solution)/shard_map/dot_general | solution.py:324
  (8 shorter events, 0.1 us)
Async XLA Ops:
  0.0 151.8 %copy-start = (bf16[2048,16]{0,1:T(8,128)(2,1)S(1)}, bf16[2048,16]{0,1:T(8,128)(2,1)}, u32[]{:S(2)}) copy-start(bf16[2048,16]{0,1:T(8,128)(2,1)} %param.15) | copy-start | bytes 196612
  0.0 62.1 %copy-start.2 = (bf16[32,8192]{1,0:T(8,128)(2,1)S(1)}, bf16[32,8192]{1,0:T(8,128)(2,1)}, u32[]{:S(2)}) copy-start(bf16[32,8192]{1,0:T(8,128)(2,1)} %param.12) | copy-start | bytes 1572868
  0.0 161.2 %collective-permute-start = (bf16[2048,256]{1,0:T(8,128)(2,1)}, bf16[2048,256]{1,0:T(8,128)(2,1)}, u32[]{:S(2)}, u32[]{:S(2)}) collective-permute-start(bf16[2048,256]{1,0:T(8,128)(2,1)} %param.16), channel_id=1, source_target_pairs={{0,1},{1,0},{2,3},{3,2},{4,5},{5,4},{6,7},{7,6},{8,9},{9,8},{10,11... | collective-permute-start | bytes 3145736 | tf_op jit(solution)/shard_map/ppermute | solution.py:259
  2.1 154.8 %collective-permute-start.2 = (bf16[2048,256]{1,0:T(8,128)(2,1)}, bf16[2048,256]{1,0:T(8,128)(2,1)}, u32[]{:S(2)}, u32[]{:S(2)}) collective-permute-start(bf16[2048,256]{1,0:T(8,128)(2,1)} %param.16), channel_id=1, source_target_pairs={{0,2},{1,3},{2,0},{3,1},{4,6},{5,7},{6,4},{7,5},{8,10},{9,11},{10,... | collective-permute-start | bytes 3145736 | tf_op jit(solution)/shard_map/ppermute | solution.py:259
  4.8 156.5 %collective-permute-start.1 = (bf16[256,2048]{1,0:T(8,128)(2,1)}, bf16[256,2048]{1,0:T(8,128)(2,1)}, u32[]{:S(2)}, u32[]{:S(2)}) collective-permute-start(bf16[256,2048]{1,0:T(8,128)(2,1)} %param.17), channel_id=1, source_target_pairs={{0,1},{1,0},{2,3},{3,2},{4,5},{5,4},{6,7},{7,6},{8,9},{9,8},{10,11... | collective-permute-start | bytes 3145736 | tf_op jit(solution)/shard_map/ppermute | solution.py:259
  6.9 152.0 %collective-permute-start.3 = (bf16[256,2048]{1,0:T(8,128)(2,1)}, bf16[256,2048]{1,0:T(8,128)(2,1)}, u32[]{:S(2)}, u32[]{:S(2)}) collective-permute-start(bf16[256,2048]{1,0:T(8,128)(2,1)} %param.17), channel_id=1, source_target_pairs={{0,2},{1,3},{2,0},{3,1},{4,6},{5,7},{6,4},{7,5},{8,10},{9,11},{10,... | collective-permute-start | bytes 3145736 | tf_op jit(solution)/shard_map/ppermute | solution.py:259
  70.6 1.0 copy-start.3
  70.6 1.0 copy-start.5
  133.2 4.0 %copy-start.1 = (bf16[64,64,128]{2,1,0:T(8,128)(2,1)S(1)}, bf16[64,64,128]{2,1,0:T(8,128)(2,1)}, u32[]{:S(2)}) copy-start(bf16[64,64,128]{2,1,0:T(8,128)(2,1)} %shard_map.101) | copy-start | bytes 3145732
  144.3 7.2 %copy-start.4 = (f32[2048]{0:T(1024)S(1)}, f32[2048]{0:T(1024)}, u32[]{:S(2)}) copy-start(f32[2048]{0:T(1024)} %param.14) | copy-start | bytes 24580
  156.9 15.1 %collective-permute-start.4 = (bf16[2048,256]{1,0:T(8,128)(2,1)}, bf16[2048,256]{1,0:T(8,128)(2,1)}, u32[]{:S(2)}, u32[]{:S(2)}) collective-permute-start(bf16[2048,256]{1,0:T(8,128)(2,1)} %collective-permute-done.2), channel_id=1, source_target_pairs={{0,1},{1,0},{2,3},{3,2},{4,5},{5,4},{6,7},{7,6},{8,9},{9,8},{10,11... | collective-permute-start | bytes 3145736 | tf_op jit(solution)/shard_map/ppermute | solution.py:259
  159.0 13.1 %collective-permute-start.5 = (bf16[256,2048]{1,0:T(8,128)(2,1)}, bf16[256,2048]{1,0:T(8,128)(2,1)}, u32[]{:S(2)}, u32[]{:S(2)}) collective-permute-start(bf16[256,2048]{1,0:T(8,128)(2,1)} %collective-permute-done.3), channel_id=1, source_target_pairs={{0,1},{1,0},{2,3},{3,2},{4,5},{5,4},{6,7},{7,6},{8,9},{9,8},{10,11... | collective-permute-start | bytes 3145736 | tf_op jit(solution)/shard_map/ppermute | solution.py:259

commit v2 on v0

v2 whole, which is shorter than its diff:
```python
import functools
import math

import jax
import jax.numpy as jnp
import numpy as np
from jax import lax
from jax.experimental import pallas as pl
from jax.experimental.pallas import tpu as pltpu
from jax.sharding import PartitionSpec as P

MESH = pl.DeviceIdType.MESH
F32, BF16 = jnp.float32, jnp.bfloat16
N = 64
GRP = 8


def class_of(dev):
    z, x, core = dev // 8, dev // 2 % 4, dev % 2
    return (x + x // 2) % 2 * 2 + core, z * 2 + x // 2


def owner_class(dev):
    x, core = dev // 2 % 4, dev % 2
    return (x + x // 2) % 2 * 2 + core


def source_of(dev, rank):
    x, core = dev // 2 % 4, dev % 2
    parity = (x + x // 2) % 2
    return (rank // 2 * 4 + parity + rank % 2 * (3 - 2 * parity)) * 2 + core


def holder_of(dev, expert):
    x, core = dev // 2 % 4, dev % 2
    pair = expert % 2
    return (expert // 2 * 4 + 2 * pair + (x + x // 2 + pair) % 2) * 2 + core


def split(table):
    high = table.astype(np.float32).astype(BF16)
    low = (table - high.astype(np.float64)).astype(np.float32).astype(BF16)
    return high, low


@functools.lru_cache(None)
def tables():
    place = np.arange(N)
    parity, core, rank = place // 32, place // 16 % 2, place % 16
    order = (rank // 2 * 4 + parity + rank % 2 * (3 - 2 * parity)) * 2 + core
    quarter = 4 * np.arange(64) + 1
    lane = np.arange(128)

    def angle(first, second, period):
        return 2.0 * math.pi * (np.outer(first, second) % period) / period

    twist = angle(quarter, lane, 32768)
    inner = angle(lane, lane, 128)
    ci, si = np.cos(inner), np.sin(inner)
    out = {"twist": np.stack([np.cos(twist), np.sin(twist)]).astype(np.float32)}
    for name, blocks in (("filt", np.arange(64)), ("sig", order)):
        theta = angle(quarter, blocks, 256)
        high, low = split(np.concatenate([np.cos(theta), -np.sin(theta)], axis=0))
        out["outer_" + name] = np.concatenate([high, low], axis=1)
    theta = angle(order, quarter, 256)
    high, low = split(np.concatenate([np.cos(theta), -np.sin(theta)], axis=1) / 8192.0)
    out["outer_inv"] = np.concatenate([high, low, high], axis=1)
    out["inner"] = np.stack(
        split(np.block([[ci, -si], [si, ci]])) + split(np.block([[ci, si], [-si, ci]])))
    return out


def dot(left, right):
    return jnp.dot(left, right, preferred_element_type=F32)


def halves(value):
    high = value.astype(BF16)
    return high, (value - high.astype(F32)).astype(BF16)


def kernel(
    tokens, target, chan, filt, gain_ffn, router, w_up, w_down,
    twist, outer_filt, outer_sig, outer_inv, inner,
    out,
    toks_t, aux, toks, auxes, stage, spec, high, low, diag, packed, rows, mid, ffn_in, hidden,
    out_rows, arrived, up, down,
    s_tok, r_tok, s_aux, r_aux, s_row, r_row, s_out, r_out, s_w, r_w, local,
):
    me = lax.axis_index("ctx")
    grp = lax.axis_index("grp")
    group, my_rank = class_of(me)
    place = group * 16 + my_rank
    expert = me // 4
    partner = me // 2 * 2 + 1 - me % 2
    across = me // 4 * 4 + (me + 2) % 4
    ahead, behind = lax.rem(grp + 1, GRP), lax.rem(grp + GRP - 1, GRP)

    barrier = pltpu.get_barrier_semaphore()

    def greet(i, carry):
        pl.semaphore_signal(
            barrier, inc=1, device_id={"ctx": lax.rem(me + i, N)}, device_id_type=MESH)
        return carry

    lax.fori_loop(1, N, greet, 0)
    for neighbour in (ahead, behind):
        pl.semaphore_signal(barrier, inc=1, device_id={"grp": neighbour}, device_id_type=MESH)

    own_up = pltpu.make_async_copy(w_up, up.at[0], local.at[0])
    own_down = pltpu.make_async_copy(w_down, down.at[pl.ds(0, 256)], local.at[1])
    own_up.start()
    own_down.start()

    total = jnp.zeros((1, 128), F32)
    for j in range(16):
        block = tokens[:, 128 * j : 128 * j + 128].astype(F32).T
        total = total + jnp.sum(block * block, axis=0, keepdims=True)
        toks_t[4 * j : 4 * j + 4] = block.astype(BF16).reshape(4, 32, 128)
    aux[0:1, :] = lax.rsqrt(total * (1.0 / 2048.0) + 1e-06)
    aux[1:2, :] = target[...]
    pl.semaphore_wait(barrier, N + 1)

    def tok_copy(peer, slot):
        return pltpu.make_async_remote_copy(
            toks_t.at[peer], toks.at[place], s_tok.at[peer], r_tok.at[slot],
            device_id={"ctx": peer}, device_id_type=MESH)

    def aux_copy(peer, slot):
        return pltpu.make_async_remote_copy(
            aux, auxes.at[place], s_aux.at[peer], r_aux.at[slot],
            device_id={"ctx": peer}, device_id_type=MESH)

    def send_toks(i, carry):
        peer = lax.rem(me + i, N)
        aux_copy(peer, me).start()
        tok_copy(peer, me).start()
        return carry

    lax.fori_loop(1, N, send_toks, 0)

    def eighth(source_up, source_down, idx, device, sems):
        ups = pl.ds(idx * 256, 256)
        return [
            pltpu.make_async_remote_copy(
                source_up.at[ups], up.at[2, ups], s_w.at[sems], r_w.at[sems],
                device_id=device, device_id_type=MESH),
            pltpu.make_async_remote_copy(
                source_down(idx), down.at[pl.ds(512 + idx * 32, 32)], s_w.at[sems + 1],
                r_w.at[sems + 1], device_id=device, device_id_type=MESH),
        ]

    def start(copies):
        for copy in copies:
            copy.start()

    def wait(copies):
        for copy in copies:
            copy.wait()

    over_x = eighth(w_up, lambda i: w_down.at[pl.ds(i * 32, 32)], grp, {"ctx": across}, 0)
    start(over_x)
    on_chip = [
        pltpu.make_async_remote_copy(
            w_up, up.at[1], s_w.at[2], r_w.at[2], device_id={"ctx": partner},
            device_id_type=MESH),
        pltpu.make_async_remote_copy(
            w_down, down.at[pl.ds(256, 256)], s_w.at[3], r_w.at[3],
            device_id={"ctx": partner}, device_id_type=MESH),
    ]
    start(on_chip)

    def held(i):
        return down.at[pl.ds(512 + i * 32, 32)]

    def ring(step):
        forth = eighth(up.at[2], held, lax.rem(grp + GRP - step, GRP), {"grp": ahead}, 4 + 4 * step)
        if step == 3:
            return forth
        return forth + eighth(
            up.at[2], held, lax.rem(grp + step, GRP), {"grp": behind}, 6 + 4 * step)

    def transform(outer):
        def channels(i, carry):
            for j in range(4):
                at = pl.multiple_of((4 * i + j) * 64, 64)
                block = stage[pl.ds(at, 64), :].astype(BF16)
                first = dot(outer[...], jnp.concatenate([block, block], axis=0))
                re, im = first[:64], first[64:]
                ct, st = twist[0], twist[1]
                re_h, re_l = halves(re * ct + im * st)
                im_h, im_l = halves(im * ct - re * st)
                high[pl.ds(at, 64), 0:128] = re_h
                high[pl.ds(at, 64), 128:256] = im_h
                low[pl.ds(at, 64), 0:128] = re_l
                low[pl.ds(at, 64), 128:256] = im_l
            return carry

        lax.fori_loop(0, 8, channels, 0)

    def inner_dot(hi, lo, which):
        return dot(hi, inner[which]) + dot(hi, inner[which + 1]) + dot(lo, inner[which])

    def load_filter(i, carry):
        stage[pl.ds(i, 32, stride=64), :] = filt[
            :, pl.ds(pl.multiple_of(i * 128, 128), 128)].astype(F32)
        return carry

    lax.fori_loop(0, N, load_filter, 0)
    transform(outer_filt)

    def filter_inner(i, carry):
        at = pl.ds(pl.multiple_of(i * 512, 512), 512)
        spec[at, :] = inner_dot(high[at, :], low[at, :], 0)
        return carry

    lax.fori_loop(0, 4, filter_inner, 0)
    wait(over_x)
    start(ring(0))

    toks[pl.ds(place, 1)] = toks_t[pl.ds(me, 1)]
    auxes[pl.ds(place, 1)] = aux[...].reshape(1, 2, 128)

    def arrive(i, carry):
        peer = lax.rem(me + N - i, N)
        aux_copy(peer, peer).wait_recv()
        tok_copy(peer, peer).wait_recv()
        return carry

    lax.fori_loop(1, N, arrive, 0)

    def normed_of(i):
        tok = toks[i].astype(F32)
        return tok, (tok * auxes[i, 0:1, :] * chan[0]).astype(BF16).astype(F32)

    def load_signal(i, carry):
        stage[pl.ds(i, 32, stride=64), :] = normed_of(i)[1]
        return carry

    lax.fori_loop(0, N, load_signal, 0)
    wait(ring(0))
    start(ring(1))
    transform(outer_sig)

    def convolve(i, carry):
        at = pl.ds(pl.multiple_of(i * 512, 512), 512)
        sig = inner_dot(high[at, :], low[at, :], 0)
        fil = spec[at, :]
        s_re, s_im = sig[:, :128], sig[:, 128:]
        f_re, f_im = fil[:, :128], fil[:, 128:]
        prod = jnp.concatenate([s_re * f_re - s_im * f_im, s_re * f_im + s_im * f_re], axis=1)
        p_h, p_l = halves(prod)
        back = inner_dot(p_h, p_l, 2)
        for j in range(8):
            re, im = back[64 * j : 64 * j + 64, :128], back[64 * j : 64 * j + 64, 128:]
            ct, st = twist[0], twist[1]
            t_h, t_l = halves(jnp.concatenate([re * ct - im * st, im * ct + re * st], axis=0))
            stage[pl.ds(pl.multiple_of(i * 512 + 64 * j, 64), 64), :] = dot(
                outer_inv[...], jnp.concatenate([t_h, t_h, t_l], axis=0))
        return carry

    lax.fori_loop(0, 4, convolve, 0)
    wait(ring(1))
    start(ring(2))

    diag[...] = jnp.zeros_like(diag)
    slot_ids = lax.broadcasted_iota(jnp.int32, (256, 128), 0).astype(F32)

    def pack(i, carry):
        picks = []
        for j in range(4):
            idx = 4 * i + j
            tok, normed = normed_of(idx)
            conv = stage[pl.ds(idx, 32, stride=64), :]
            conv_out = (conv + chan[1] * normed).astype(BF16).astype(F32)
            diag[32 * j : 32 * j + 32, 128 * j : 128 * j + 128] = (tok + conv_out).astype(BF16)
            picks.append(jnp.where(slot_ids == auxes[idx, 1:2, :], 1.0, 0.0).astype(BF16))
        picked = lax.dot_general(
            jnp.concatenate(picks, axis=1), diag[...], (((1,), (1,)), ((), ())),
            preferred_element_type=F32)
        packed[i // 4, :, pl.ds(pl.multiple_of(i % 4 * 16, 16), 16), :] = (
            picked.astype(BF16).reshape(16, 16, 128))
        return carry

    lax.fori_loop(0, 16, pack, 0)

    def row_copy(peer, slot):
        return pltpu.make_async_remote_copy(
            packed.at[owner_class(peer), peer // 4], rows.at[me], s_row.at[peer], r_row.at[slot],
            device_id={"ctx": peer}, device_id_type=MESH)

    def send_rows(i, carry):
        row_copy(lax.rem(me + i, N), me).start()
        return carry

    lax.fori_loop(1, N, send_rows, 0)
    wait(ring(2))
    start(ring(3))
    rows[pl.ds(me, 1)] = packed[group, pl.ds(expert, 1)]
    wait(ring(3))
    relay = [
        pltpu.make_async_remote_copy(
            up.at[2], up.at[3], s_w.at[18], r_w.at[18], device_id={"ctx": partner},
            device_id_type=MESH),
        pltpu.make_async_remote_copy(
            down.at[pl.ds(512, 256)], down.at[pl.ds(768, 256)], s_w.at[19], r_w.at[19],
            device_id={"ctx": partner}, device_id_type=MESH),
    ]
    start(relay)

    def rows_arrive(i, carry):
        peer = lax.rem(me + N - i, N)
        row_copy(peer, peer).wait_recv()
        return carry

    lax.fori_loop(1, N, rows_arrive, 0)

    lane = lax.broadcasted_iota(jnp.int32, (16, 128), 1)
    in_half, in_quarter = lane < 64, lane % 64 < 32

    def unpack(i, carry):
        at = pl.ds(pl.multiple_of(i * 128, 128), 128)
        for r in range(4):
            v = [rows[4 * i + j, 16 * r : 16 * r + 16, :].astype(F32) for j in range(4)]
            a0 = jnp.where(in_half, v[0], pltpu.roll(v[2], 64, 1))
            a1 = jnp.where(in_half, v[1], pltpu.roll(v[3], 64, 1))
            a2 = jnp.where(in_half, pltpu.roll(v[0], 64, 1), v[2])
            a3 = jnp.where(in_half, pltpu.roll(v[1], 64, 1), v[3])
            u = [
                jnp.where(in_quarter, a0, pltpu.roll(a1, 32, 1)),
                jnp.where(in_quarter, pltpu.roll(a0, 96, 1), a1),
                jnp.where(in_quarter, a2, pltpu.roll(a3, 32, 1)),
                jnp.where(in_quarter, pltpu.roll(a2, 96, 1), a3),
            ]
            for p in range(4):
                mid[64 * r + 16 * p : 64 * r + 16 * p + 16, at] = u[p]
        return carry

    lax.fori_loop(0, 16, unpack, 0)

    def norm_rows(i, carry):
        at = pl.ds(pl.multiple_of(i * 32, 32), 32)
        block = mid[at, :]
        scale = lax.rsqrt(
            jnp.sum(block * block, axis=1, keepdims=True) * (1.0 / 2048.0) + 1e-06)
        ffn_in[at, :] = (block * scale * gain_ffn[...]).astype(BF16)
        return carry

    lax.fori_loop(0, 8, norm_rows, 0)
    logits = dot(ffn_in[...], router[...])
    chosen = lax.broadcasted_iota(jnp.int32, logits.shape, 1) == expert
    gate = jax.nn.sigmoid(jnp.sum(jnp.where(chosen, logits, 0.0), axis=1, keepdims=True))

    own_up.wait()
    own_down.wait()
    wait(on_chip)
    wait(relay)

    def go_up(i, carry):
        value = dot(ffn_in[...], up[i])
        value = value * (1.0 + lax.erf(value * math.sqrt(0.5))) * 0.5
        hidden[:, pl.ds(pl.multiple_of(i * 256, 256), 256)] = value.astype(BF16)
        return carry

    lax.fori_loop(0, 4, go_up, 0)

    def go_down(i, carry):
        at = pl.ds(pl.multiple_of(i * 256, 256), 256)
        result = dot(hidden[...], down[:, at]).astype(BF16).astype(F32)
        out_rows[:, :, at] = (mid[:, at] + gate * result).astype(BF16).reshape(16, 16, 256)
        return carry

    lax.fori_loop(0, 8, go_down, 0)

    def out_copy(rank, slot):
        return pltpu.make_async_remote_copy(
            out_rows.at[rank], arrived.at[expert], s_out.at[rank], r_out.at[slot],
            device_id={"ctx": source_of(me, rank)}, device_id_type=MESH)

    def send_out(rank, carry):
        @pl.when(source_of(me, rank) != me)
        def _():
            out_copy(rank, expert).start()
        return carry

    lax.fori_loop(0, 16, send_out, 0)

    @pl.when(source_of(me, my_rank) == me)
    def _():
        arrived[pl.ds(expert, 1)] = out_rows[pl.ds(my_rank, 1)]

    pick = jnp.where(slot_ids == target[...], 1.0, 0.0).T.astype(BF16)

    def out_arrive(i, carry):
        @pl.when(holder_of(me, i) != me)
        def _():
            out_copy(0, i).wait_recv()
        return carry

    lax.fori_loop(0, 16, out_arrive, 0)

    def select(i, carry):
        at = pl.ds(pl.multiple_of(i * 256, 256), 256)
        out[:, at] = dot(pick, arrived[:, :, at].reshape(256, 256)).astype(BF16)
        return carry

    lax.fori_loop(0, 8, select, 0)

    def sent(i, carry):
        peer = lax.rem(me + i, N)
        aux_copy(peer, peer).wait_send()
        tok_copy(peer, peer).wait_send()
        row_copy(peer, peer).wait_send()
        return carry

    lax.fori_loop(1, N, sent, 0)

    def sent_out(rank, carry):
        @pl.when(source_of(me, rank) != me)
        def _():
            out_copy(rank, rank).wait_send()
        return carry

    lax.fori_loop(0, 16, sent_out, 0)


def body(
    tokens, gain_in, long_filter, skip_gain, gain_ffn, router, w_up, w_down, expert_id, slot_index
):
    me = lax.axis_index("ctx")
    target = (expert_id * 16 + slot_index).astype(F32).reshape(1, 128)
    gain = lax.dynamic_slice(gain_in, (me * 32,), (32,))
    chan = jnp.broadcast_to(jnp.stack([gain, skip_gain])[:, :, None], (2, 32, 128))
    t = tables()
    consts = [jnp.asarray(t[k]) for k in ("twist", "outer_filt", "outer_sig", "outer_inv", "inner")]
    vmem = pl.BlockSpec(memory_space=pltpu.VMEM)
    anywhere = pl.BlockSpec(memory_space=pl.ANY)
    dma = pltpu.SemaphoreType.DMA
    return pl.pallas_call(
        kernel,
        out_shape=jax.ShapeDtypeStruct((128, 2048), BF16),
        in_specs=[vmem] * 6 + [anywhere] * 2 + [vmem] * 5,
        out_specs=vmem,
        scratch_shapes=[
            pltpu.VMEM((N, 32, 128), BF16),
            pltpu.VMEM((2, 128), F32),
            pltpu.VMEM((N, 32, 128), BF16),
            pltpu.VMEM((N, 2, 128), F32),
            pltpu.VMEM((2048, 128), F32),
            pltpu.VMEM((2048, 256), F32),
            pltpu.VMEM((2048, 256), BF16),
            pltpu.VMEM((2048, 256), BF16),
            pltpu.VMEM((128, 512), BF16),
            pltpu.VMEM((4, 16, 64, 128), BF16),
            pltpu.VMEM((N, 64, 128), BF16),
            pltpu.VMEM((256, 2048), F32),
            pltpu.VMEM((256, 2048), BF16),
            pltpu.VMEM((256, 1024), BF16),
            pltpu.VMEM((16, 16, 2048), BF16),
            pltpu.VMEM((16, 16, 2048), BF16),
            pltpu.VMEM((4, 2048, 256), BF16),
            pltpu.VMEM((1024, 2048), BF16),
            dma((N,)), dma((N,)), dma((N,)), dma((N,)), dma((N,)), dma((N,)),
            dma((16,)), dma((16,)), dma((20,)), dma((20,)), dma((2,)),
        ],
        compiler_params=pltpu.CompilerParams(
            collective_id=0, has_side_effects=True, vmem_limit_bytes=60 * 1024 * 1024),
    )(
        tokens, target, chan, long_filter, gain_ffn.reshape(1, 2048), router, w_up, w_down, *consts
    )


def solution(mesh):
    return jax.shard_map(
        body,
        mesh=mesh,
        in_specs=(
            P(("grp", "ctx"), None),
            P(),
            P("ctx", None),
            P("ctx"),
            P(),
            P(),
            P(None, "ctx"),
            P("ctx", None),
            P(("grp", "ctx")),
            P(("grp", "ctx")),
        ),
        out_specs=P(("grp", "ctx"), None),
        check_vma=False,
    )
```

time: 282 us -> 119 us (0.42)
  the two profiles are of different devices: /device:TPU:6 before, /device:TPU:128 now
where the time goes in v2:
time: 119 us
  Pallas kernels  112 us (94%)
  local copies, waits for them, and re-layouts  6.41 us (5%)
    pallas_call x1, Pallas kernels, body(): pl.pallas_call(kernel, out_shape=jax.ShapeDtypeStruct((128, 2048), BF16),...  112 us
    unnamed x10, local copies, waits for them, and re-layouts  5.66 us

profile of v2, /device:TPU:128, one launch (start us, length us, event | category | flops | bytes accessed | tf_op | source)
XLA Modules:
  0.0 119.1 jit_solution(15102031470167691886)
XLA Ops:
  0.0 0.0 copy-start
  0.0 0.7 copy-done
  0.7 0.0 copy-start.1
  0.7 0.1 dynamic-slice_bitcast_fusion
  0.8 0.6 copy-done.1
  1.4 0.0 copy-start.2
  1.4 0.0 copy-start.3
  1.4 0.6 copy-done.2
  2.0 0.0 copy-done.3
  2.0 0.6 convert_bitcast_fusion.target
  2.6 0.7 broadcast_in_dim.2.chan
  3.3 1.8 %copy.16.router = bf16[2048,16]{1,0:T(8,128)(2,1)} copy(bf16[2048,16]{0,1:T(8,128)(2,1)} %param.20) | data formatting | bytes 131072 | tf_op args[5]
  5.1 112.1 %shard_map.145 = bf16[128,2048]{1,0:T(8,128)(2,1)} custom-call(bf16[128,2048]{1,0:T(8,128)(2,1)} %tokens.1, f32[1,128]{1,0:T(1,128)} %convert_bitcast_fusion.target, f32[2,32,128]{2,1,0:T(8,128)} %broadcast_in_dim.2.chan, bf16[32,8192]{1,0:T(8,128)(2,1)} %filt.1, f32[1,2048]{1,0:T(1,128)} %bitcast.6, bf16[2048,16]{1,0:T(8,128)(2,1)} %copy.16.router, ...), custom_call_target="tpu_custom_call" | custom-call | tf_op jit(solution)/shard_map/pallas_call | solution.py:439
  117.3 1.9 %copy.18 = bf16[128,2048]{1,0:T(8,128)(2,1)} copy(bf16[128,2048]{1,0:T(8,128)(2,1)} %shard_map.145) | data formatting | bytes 1048576
  (1 shorter events, 0.0 us)
Async XLA Ops:
  0.0 0.7 copy-start
  0.7 0.7 copy-start.1
  1.4 0.7 copy-start.2
  1.4 0.7 copy-start.3

commit v3 on v2

v3 whole, which is shorter than its diff:
```python
import functools
import math

import jax
import jax.numpy as jnp
import numpy as np
from jax import lax
from jax.experimental import pallas as pl
from jax.experimental.pallas import tpu as pltpu
from jax.sharding import PartitionSpec as P

MESH = pl.DeviceIdType.MESH
F32, BF16 = jnp.float32, jnp.bfloat16
N = 64
GRP = 8


def class_of(dev):
    z, x, core = dev // 8, dev // 2 % 4, dev % 2
    return (x + x // 2) % 2 * 2 + core, x // 2 * 8 + z


def source_of(dev, rank):
    x, core = dev // 2 % 4, dev % 2
    parity = (x + x // 2) % 2
    return (rank % 8 * 4 + parity + rank // 8 * (3 - 2 * parity)) * 2 + core


def holder_of(group, expert):
    parity, core, pair = group // 2, group % 2, expert % 2
    return (expert // 2 * 4 + 2 * pair + (parity + pair) % 2) * 2 + core


def split(table):
    high = table.astype(np.float32).astype(BF16)
    low = (table - high.astype(np.float64)).astype(np.float32).astype(BF16)
    return high, low


@functools.lru_cache(None)
def tables():
    place = np.arange(N)
    parity, core, rank = place // 32, place // 16 % 2, place % 16
    order = (rank % 8 * 4 + parity + rank // 8 * (3 - 2 * parity)) * 2 + core
    quarter = 4 * np.arange(64) + 1
    lane = np.arange(128)

    def angle(first, second, period):
        return 2.0 * math.pi * (np.outer(first, second) % period) / period

    twist = angle(quarter, lane, 32768)
    inner = angle(lane, lane, 128)
    ci, si = np.cos(inner), np.sin(inner)
    out = {"twist": np.stack([np.cos(twist), np.sin(twist)]).astype(np.float32)}
    for name, blocks in (("filt", np.arange(64)), ("sig", order)):
        theta = angle(quarter, blocks, 256)
        high, low = split(np.concatenate([np.cos(theta), -np.sin(theta)], axis=0))
        out["outer_" + name] = np.concatenate([high, low], axis=1)
    theta = angle(order, quarter, 256)
    high, low = split(np.concatenate([np.cos(theta), -np.sin(theta)], axis=1) / 8192.0)
    out["outer_inv"] = np.concatenate([high, low, high], axis=1)
    out["inner"] = np.stack(
        split(np.block([[ci, -si], [si, ci]])) + split(np.block([[ci, si], [-si, ci]])))
    return out


def dot(left, right):
    return jnp.dot(left, right, preferred_element_type=F32)


def halves(value):
    high = value.astype(BF16)
    return high, (value - high.astype(F32)).astype(BF16)


def settle(ref, sem):
    pltpu.make_async_copy(ref, ref, sem).wait()


def kernel(
    tokens, expert_id, slot_index, chan, filt_hbm, gain_ffn, router, w_up, w_down,
    twist, outer_filt, outer_sig, outer_inv, inner_hbm,
    out,
    toks_t, aux, toks, auxes, filt, inner, stage, spec, high, low, diag, packed, rows, mid,
    ffn_in, hidden, out_rows, arrived, up, down,
    s_tok, r_tok, s_aux, r_aux, s_row, r_row, s_out, r_out, s_w, r_w, local,
):
    me = lax.axis_index("ctx")
    grp = lax.axis_index("grp")
    group, my_rank = class_of(me)
    place = group * 16 + my_rank
    expert = me // 4
    partner = me // 2 * 2 + 1 - me % 2
    across = me // 4 * 4 + (me + 2) % 4
    ahead, behind = lax.rem(grp + 1, GRP), lax.rem(grp + GRP - 1, GRP)
    ahead2, behind2 = lax.rem(grp + 2, GRP), lax.rem(grp + GRP - 2, GRP)

    barrier = pltpu.get_barrier_semaphore()

    def greet(i, carry):
        pl.semaphore_signal(
            barrier, inc=1, device_id={"ctx": lax.rem(me + i, N)}, device_id_type=MESH)
        return carry

    lax.fori_loop(1, N, greet, 0)
    for neighbour in (ahead, behind, ahead2, behind2):
        pl.semaphore_signal(barrier, inc=1, device_id={"grp": neighbour}, device_id_type=MESH)

    fetches = [
        pltpu.make_async_copy(filt_hbm, filt, local.at[0]),
        pltpu.make_async_copy(inner_hbm, inner, local.at[1]),
        pltpu.make_async_copy(w_up, up.at[0], local.at[2]),
        pltpu.make_async_copy(w_down, down.at[pl.ds(0, 256)], local.at[3]),
    ]
    for fetch in fetches:
        fetch.start()

    total = jnp.zeros((1, 128), F32)
    for j in range(16):
        block = tokens[:, 128 * j : 128 * j + 128].astype(F32).T
        total = total + jnp.sum(block * block, axis=0, keepdims=True)
        toks_t[4 * j : 4 * j + 4] = block.astype(BF16).reshape(4, 32, 128)
    target = (expert_id[...] * 16 + slot_index[...]).astype(F32)
    aux[0:1, :] = lax.rsqrt(total * (1.0 / 2048.0) + 1e-06)
    aux[1:2, :] = target
    pl.semaphore_wait(barrier, N + 3)

    def push(source, dest, sem, device):
        pltpu.make_async_remote_copy(
            source, dest, s_w.at[sem], r_w.at[sem], device_id=device, device_id_type=MESH
        ).start()

    quarter = lax.rem(grp, 4)
    up_at = pl.multiple_of(quarter * 512, 512)
    down_at = pl.multiple_of(quarter * 64, 64)

    def held_up(first, count):
        return up.at[2, pl.ds(up_at + first, count)]

    def held_down(first, count):
        return down.at[pl.ds(512 + down_at + first, count)]

    push(w_up.at[pl.ds(up_at, 512)], held_up(0, 512), 0, {"ctx": across})
    push(w_down.at[pl.ds(down_at, 64)], held_down(0, 64), 1, {"ctx": across})

    def send_toks(half):
        def send(i, carry):
            peer = lax.rem(me + i, N)
            if half == 0:
                pltpu.make_async_remote_copy(
                    aux, auxes.at[place], s_aux, r_aux, device_id={"ctx": peer},
                    device_id_type=MESH).start()
            channels = pl.ds(16 * half, 16)
            pltpu.make_async_remote_copy(
                toks_t.at[peer, channels], toks.at[place, channels], s_tok.at[half],
                r_tok.at[half], device_id={"ctx": peer}, device_id_type=MESH).start()
            return carry

        lax.fori_loop(1, N, send, 0)

    send_toks(0)
    send_toks(1)
    push(w_up, up.at[1], 2, {"ctx": partner})
    push(w_down, down.at[pl.ds(256, 256)], 3, {"ctx": partner})
    toks[pl.ds(place, 1)] = toks_t[pl.ds(me, 1)]
    auxes[pl.ds(place, 1)] = aux[...].reshape(1, 2, 128)

    def transform(outer, begin, end):
        def channels(i, carry):
            for j in range(4):
                at = pl.multiple_of((4 * i + j) * 64, 64)
                block = stage[pl.ds(at, 64), :].astype(BF16)
                first = dot(outer[...], jnp.concatenate([block, block], axis=0))
                re, im = first[:64], first[64:]
                ct, st = twist[0], twist[1]
                re_h, re_l = halves(re * ct + im * st)
                im_h, im_l = halves(im * ct - re * st)
                high[pl.ds(at, 64), 0:128] = re_h
                high[pl.ds(at, 64), 128:256] = im_h
                low[pl.ds(at, 64), 0:128] = re_l
                low[pl.ds(at, 64), 128:256] = im_l
            return carry

        lax.fori_loop(begin, end, channels, 0)

    def inner_dot(hi, lo, which):
        return dot(hi, inner[which]) + dot(hi, inner[which + 1]) + dot(lo, inner[which])

    def load_filter(i, carry):
        stage[pl.ds(i, 32, stride=64), :] = filt[
            :, pl.ds(pl.multiple_of(i * 128, 128), 128)].astype(F32)
        return carry

    fetches[0].wait()
    fetches[1].wait()
    lax.fori_loop(0, N, load_filter, 0)
    transform(outer_filt, 0, 8)

    def filter_inner(i, carry):
        at = pl.ds(pl.multiple_of(i * 512, 512), 512)
        spec[at, :] = inner_dot(high[at, :], low[at, :], 0)
        return carry

    lax.fori_loop(0, 4, filter_inner, 0)

    settle(held_up(0, 512), r_w.at[0])
    settle(held_down(0, 64), r_w.at[1])
    for first, device in ((0, ahead2), (1, behind2)):
        push(held_up(256 * first, 256), held_up(256 * first, 256), 4, {"grp": device})
        push(held_down(32 * first, 32), held_down(32 * first, 32), 5, {"grp": device})
    for device in (ahead, behind):
        push(held_up(0, 512), held_up(0, 512), 4, {"grp": device})
        push(held_down(0, 64), held_down(0, 64), 5, {"grp": device})

    def convolve(i, carry):
        at = pl.ds(pl.multiple_of(i * 512, 512), 512)
        sig = inner_dot(high[at, :], low[at, :], 0)
        fil = spec[at, :]
        s_re, s_im = sig[:, :128], sig[:, 128:]
        f_re, f_im = fil[:, :128], fil[:, 128:]
        prod = jnp.concatenate([s_re * f_re - s_im * f_im, s_re * f_im + s_im * f_re], axis=1)
        p_h, p_l = halves(prod)
        back = inner_dot(p_h, p_l, 2)
        for j in range(8):
            re, im = back[64 * j : 64 * j + 64, :128], back[64 * j : 64 * j + 64, 128:]
            ct, st = twist[0], twist[1]
            t_h, t_l = halves(jnp.concatenate([re * ct - im * st, im * ct + re * st], axis=0))
            stage[pl.ds(pl.multiple_of(i * 512 + 64 * j, 64), 64), :] = dot(
                outer_inv[...], jnp.concatenate([t_h, t_h, t_l], axis=0))
        return carry

    settle(auxes.at[pl.ds(0, N - 1)], r_aux)
    for half in range(2):
        begin = 16 * half
        settle(toks.at[pl.ds(0, N - 1), pl.ds(begin, 16)], r_tok.at[half])

        def load_signal(i, carry):
            tok = toks[i, begin : begin + 16].astype(F32)
            normed = (tok * auxes[i, 0:1, :] * chan[0, begin : begin + 16]).astype(BF16)
            stage[pl.ds(64 * begin + i, 16, stride=64), :] = normed.astype(F32)
            return carry

        lax.fori_loop(0, N, load_signal, 0)
        transform(outer_sig, 4 * half, 4 * half + 4)
        lax.fori_loop(2 * half, 2 * half + 2, convolve, 0)

    diag[...] = jnp.zeros_like(diag)
    slot_ids = lax.broadcasted_iota(jnp.int32, (256, 128), 0).astype(F32)

    def pack(cls, part):
        picks = []
        for j in range(4):
            idx = cls * 16 + part * 4 + j
            tok = toks[idx].astype(F32)
            normed = (tok * auxes[idx, 0:1, :] * chan[0]).astype(BF16).astype(F32)
            conv = stage[pl.ds(idx, 32, stride=64), :]
            conv_out = (conv + chan[1] * normed).astype(BF16).astype(F32)
            diag[32 * j : 32 * j + 32, 128 * j : 128 * j + 128] = (tok + conv_out).astype(BF16)
            picks.append(jnp.where(slot_ids == auxes[idx, 1:2, :], 1.0, 0.0).astype(BF16))
        picked = lax.dot_general(
            jnp.concatenate(picks, axis=1), diag[...], (((1,), (1,)), ((), ())),
            preferred_element_type=F32)
        packed[cls, :, 16 * part : 16 * part + 16, :] = picked.astype(BF16).reshape(16, 16, 128)

    for half in range(2):

        def pack_class(i, carry):
            cls = lax.rem(group + i, 4)
            pack(cls, 2 * half)
            pack(cls, 2 * half + 1)
            part = pl.ds(32 * half, 32)

            def send(t, carry):
                to = lax.rem(expert + t, 16)
                dest = holder_of(cls, to)

                @pl.when(dest != me)
                def _():
                    pltpu.make_async_remote_copy(
                        packed.at[cls, to, part], rows.at[me, part], s_row.at[half],
                        r_row.at[half], device_id={"ctx": dest}, device_id_type=MESH).start()
                return carry

            lax.fori_loop(0, 16, send, 0)
            return carry

        lax.fori_loop(0, 4, pack_class, 0)

    rows[pl.ds(me, 1)] = packed[group, pl.ds(expert, 1)]

    settle(up.at[2, pl.ds(0, 1536)], r_w.at[4])
    settle(down.at[pl.ds(512, 192)], r_w.at[5])
    push(up.at[2], up.at[3], 6, {"ctx": partner})
    push(down.at[pl.ds(512, 256)], down.at[pl.ds(768, 256)], 7, {"ctx": partner})

    lane = lax.broadcasted_iota(jnp.int32, (16, 128), 1)
    in_half, in_quarter = lane < 64, lane % 64 < 32
    for half in range(2):
        part = pl.ds(32 * half, 32)
        these = pl.ds(128 * half, 128)
        settle(rows.at[pl.ds(0, N - 1), part], r_row.at[half])

        def unpack(i, carry):
            at = pl.ds(pl.multiple_of(i * 128, 128), 128)
            for r in (2 * half, 2 * half + 1):
                v = [rows[4 * i + j, 16 * r : 16 * r + 16, :].astype(F32) for j in range(4)]
                a0 = jnp.where(in_half, v[0], pltpu.roll(v[2], 64, 1))
                a1 = jnp.where(in_half, v[1], pltpu.roll(v[3], 64, 1))
                a2 = jnp.where(in_half, pltpu.roll(v[0], 64, 1), v[2])
                a3 = jnp.where(in_half, pltpu.roll(v[1], 64, 1), v[3])
                u = [
                    jnp.where(in_quarter, a0, pltpu.roll(a1, 32, 1)),
                    jnp.where(in_quarter, pltpu.roll(a0, 96, 1), a1),
                    jnp.where(in_quarter, a2, pltpu.roll(a3, 32, 1)),
                    jnp.where(in_quarter, pltpu.roll(a2, 96, 1), a3),
                ]
                for p in range(4):
                    mid[64 * r + 16 * p : 64 * r + 16 * p + 16, at] = u[p]
            return carry

        lax.fori_loop(0, 16, unpack, 0)

        def norm_rows(i, carry):
            at = pl.ds(pl.multiple_of(i * 32, 32), 32)
            block = mid[at, :]
            scale = lax.rsqrt(
                jnp.sum(block * block, axis=1, keepdims=True) * (1.0 / 2048.0) + 1e-06)
            ffn_in[at, :] = (block * scale * gain_ffn[...]).astype(BF16)
            return carry

        lax.fori_loop(4 * half, 4 * half + 4, norm_rows, 0)
        logits = lax.dot_general(
            ffn_in[these, :], router[...], (((1,), (1,)), ((), ())), preferred_element_type=F32)
        chosen = lax.broadcasted_iota(jnp.int32, logits.shape, 1) == expert
        gate = jax.nn.sigmoid(jnp.sum(jnp.where(chosen, logits, 0.0), axis=1, keepdims=True))

        if half == 0:
            fetches[2].wait()
            fetches[3].wait()
            settle(up.at[1], r_w.at[2])
            settle(down.at[pl.ds(256, 256)], r_w.at[3])
            settle(up.at[3], r_w.at[6])
            settle(down.at[pl.ds(768, 256)], r_w.at[7])

        def go_up(i, carry):
            value = dot(ffn_in[these, :], up[i])
            value = value * (1.0 + lax.erf(value * math.sqrt(0.5))) * 0.5
            hidden[these, pl.ds(pl.multiple_of(i * 256, 256), 256)] = value.astype(BF16)
            return carry

        lax.fori_loop(0, 4, go_up, 0)

        def go_down(i, carry):
            at = pl.ds(pl.multiple_of(i * 256, 256), 256)
            result = dot(hidden[these, :], down[:, at]).astype(BF16).astype(F32)
            value = (mid[these, at] + gate * result).astype(BF16)
            out_rows[8 * half : 8 * half + 8, :, at] = value.reshape(8, 16, 256)
            return carry

        lax.fori_loop(0, 8, go_down, 0)

        def send_out(i, carry):
            rank = 8 * half + lax.rem(my_rank + i, 8)

            @pl.when(rank != my_rank)
            def _():
                pltpu.make_async_remote_copy(
                    out_rows.at[rank], arrived.at[expert], s_out, r_out,
                    device_id={"ctx": source_of(me, rank)}, device_id_type=MESH).start()
            return carry

        lax.fori_loop(0, 8, send_out, 0)

    arrived[pl.ds(expert, 1)] = out_rows[pl.ds(my_rank, 1)]
    pick = jnp.where(slot_ids == target, 1.0, 0.0).T.astype(BF16)
    settle(arrived.at[pl.ds(0, 15)], r_out)

    def select(i, carry):
        at = pl.ds(pl.multiple_of(i * 256, 256), 256)
        out[:, at] = dot(pick, arrived[:, :, at].reshape(256, 256)).astype(BF16)
        return carry

    lax.fori_loop(0, 8, select, 0)

    settle(auxes.at[pl.ds(0, N - 1)], s_aux)
    for half in range(2):
        settle(toks.at[pl.ds(0, N - 1), pl.ds(16 * half, 16)], s_tok.at[half])
        settle(rows.at[pl.ds(0, N - 1), pl.ds(32 * half, 32)], s_row.at[half])
    settle(arrived.at[pl.ds(0, 15)], s_out)
    for sem, ref in enumerate((
        held_up(0, 512), held_down(0, 64), up.at[1], down.at[pl.ds(256, 256)],
        up.at[2, pl.ds(0, 1536)], down.at[pl.ds(512, 192)], up.at[3], down.at[pl.ds(768, 256)],
    )):
        settle(ref, s_w.at[sem])


def body(
    tokens, gain_in, long_filter, skip_gain, gain_ffn, router, w_up, w_down, expert_id, slot_index
):
    me = lax.axis_index("ctx")
    gain = lax.dynamic_slice(gain_in, (me * 32,), (32,))
    chan = jnp.broadcast_to(jnp.stack([gain, skip_gain])[:, :, None], (2, 32, 128))
    t = tables()
    consts = [jnp.asarray(t[k]) for k in ("twist", "outer_filt", "outer_sig", "outer_inv", "inner")]
    vmem = pl.BlockSpec(memory_space=pltpu.VMEM)
    anywhere = pl.BlockSpec(memory_space=pl.ANY)
    dma = pltpu.SemaphoreType.DMA
    return pl.pallas_call(
        kernel,
        out_shape=jax.ShapeDtypeStruct((128, 2048), BF16),
        in_specs=[vmem] * 4 + [anywhere] + [vmem] * 2 + [anywhere] * 2 + [vmem] * 4 + [anywhere],
        out_specs=vmem,
        scratch_shapes=[
            pltpu.VMEM((N, 32, 128), BF16),
            pltpu.VMEM((2, 128), F32),
            pltpu.VMEM((N, 32, 128), BF16),
            pltpu.VMEM((N, 2, 128), F32),
            pltpu.VMEM((32, 8192), BF16),
            pltpu.VMEM((4, 256, 256), BF16),
            pltpu.VMEM((2048, 128), F32),
            pltpu.VMEM((2048, 256), F32),
            pltpu.VMEM((2048, 256), BF16),
            pltpu.VMEM((2048, 256), BF16),
            pltpu.VMEM((128, 512), BF16),
            pltpu.VMEM((4, 16, 64, 128), BF16),
            pltpu.VMEM((N, 64, 128), BF16),
            pltpu.VMEM((256, 2048), F32),
            pltpu.VMEM((256, 2048), BF16),
            pltpu.VMEM((256, 1024), BF16),
            pltpu.VMEM((16, 16, 2048), BF16),
            pltpu.VMEM((16, 16, 2048), BF16),
            pltpu.VMEM((4, 2048, 256), BF16),
            pltpu.VMEM((1024, 2048), BF16),
            dma((2,)), dma((2,)), dma, dma, dma((2,)), dma((2,)), dma, dma, dma((8,)), dma((8,)),
            dma((4,)),
        ],
        compiler_params=pltpu.CompilerParams(
            collective_id=0, has_side_effects=True, vmem_limit_bytes=60 * 1024 * 1024),
    )(
        tokens, expert_id.reshape(1, 128), slot_index.reshape(1, 128), chan, long_filter,
        gain_ffn.reshape(1, 2048), router.T, w_up, w_down, *consts
    )


def solution(mesh):
    return jax.shard_map(
        body,
        mesh=mesh,
        in_specs=(
            P(("grp", "ctx"), None),
            P(),
            P("ctx", None),
            P("ctx"),
            P(),
            P(),
            P(None, "ctx"),
            P("ctx", None),
            P(("grp", "ctx")),
            P(("grp", "ctx")),
        ),
        out_specs=P(("grp", "ctx"), None),
        check_vma=False,
    )
```

time: 119 us -> 101 us (0.85)
  the two profiles are of different devices: /device:TPU:128 before, /device:TPU:6 now
where the time goes in v3:
time: 101 us; the launch traced here: 100 us
  Pallas kernels  96.5 us (96%)
  local copies, waits for them, and re-layouts  3.92 us (4%)
    pallas_call x1, Pallas kernels, body(): pl.pallas_call(kernel, out_shape=jax.ShapeDtypeStruct((128, 2048), BF16),...  96.5 us
    unnamed x5, local copies, waits for them, and re-layouts  3.16 us

profile of v3, /device:TPU:6, one launch (start us, length us, event | category | flops | bytes accessed | tf_op | source)
XLA Modules:
  0.0 100.4 jit_solution(10692329049119273179)
XLA Ops:
  0.0 0.0 copy-start
  0.0 0.7 copy-done
  0.7 0.0 copy-start.1
  0.7 0.1 dynamic-slice_bitcast_fusion
  0.8 0.6 copy-done.1
  1.4 0.7 broadcast_in_dim.2.chan
  2.1 96.5 %shard_map.145 = bf16[128,2048]{1,0:T(8,128)(2,1)} custom-call(bf16[128,2048]{1,0:T(8,128)(2,1)} %tokens.1, s32[1,128]{1,0:T(1,128)} %bitcast.9, s32[1,128]{1,0:T(1,128)} %bitcast.10, f32[2,32,128]{2,1,0:T(8,128)} %broadcast_in_dim.2.chan, bf16[32,8192]{1,0:T(8,128)(2,1)} %filt_hbm.1, f32[1,2048]{1,0:T(1,128)} %bitcast.8, bf16[16,2048]{1,0:T(8,128)(2,1)} %bitcast.7, ...), custom_call_target="tpu_custom_call" | custom-call | tf_op jit(solution)/shard_map/pallas_call | solution.py:408
  98.5 1.9 %copy.17 = bf16[128,2048]{1,0:T(8,128)(2,1)} copy(bf16[128,2048]{1,0:T(8,128)(2,1)} %shard_map.145) | data formatting | bytes 1048576
  (1 shorter events, 0.0 us)
Async XLA Ops:
  0.0 0.7 copy-start
  0.7 0.7 copy-start.1

commit v4 on v3

--- a/solution.py
+++ b/solution.py
@@ -13,17 +13,20 @@
 F32, BF16 = jnp.float32, jnp.bfloat16
 N = 64
 GRP = 8
+PARTS = 2
+WIDE = 32 // PARTS
 
 
 def class_of(dev):
     z, x, core = dev // 8, dev // 2 % 4, dev % 2
-    return (x + x // 2) % 2 * 2 + core, x // 2 * 8 + z
+    return (x + x // 2) % 2 * 2 + core, (x // 2 + z) % 2 * 8 + z
 
 
 def source_of(dev, rank):
     x, core = dev // 2 % 4, dev % 2
     parity = (x + x // 2) % 2
-    return (rank % 8 * 4 + parity + rank // 8 * (3 - 2 * parity)) * 2 + core
+    side = (rank // 8 + rank) % 2
+    return (rank % 8 * 4 + parity + side * (3 - 2 * parity)) * 2 + core
 
 
 def holder_of(group, expert):
@@ -41,7 +44,8 @@
 def tables():
     place = np.arange(N)
     parity, core, rank = place // 32, place // 16 % 2, place % 16
-    order = (rank % 8 * 4 + parity + rank // 8 * (3 - 2 * parity)) * 2 + core
+    side = (rank // 8 + rank) % 2
+    order = (rank % 8 * 4 + parity + side * (3 - 2 * parity)) * 2 + core
     quarter = 4 * np.arange(64) + 1
     lane = np.arange(128)
 
@@ -78,12 +82,12 @@
 
 
 def kernel(
-    tokens, expert_id, slot_index, chan, filt_hbm, gain_ffn, router, w_up, w_down,
+    tokens, expert_id, slot_index, gain_in, skip_gain, filt_hbm, gain_ffn, router, w_up, w_down,
     twist, outer_filt, outer_sig, outer_inv, inner_hbm,
     out,
-    toks_t, aux, toks, auxes, filt, inner, stage, spec, high, low, diag, packed, rows, mid,
+    chan, turned_gain, toks_t, aux, toks, scales, targets, filt, inner, stage, spec, high, low, diag, packed, rows, mid,
     ffn_in, hidden, out_rows, arrived, up, down,
-    s_tok, r_tok, s_aux, r_aux, s_row, r_row, s_out, r_out, s_w, r_w, local,
+    s_tok, r_tok, s_aux, r_aux, s_tgt, r_tgt, s_row, r_row, s_out, r_out, s_w, r_w, local,
 ):
     me = lax.axis_index("ctx")
     grp = lax.axis_index("grp")
@@ -121,8 +125,12 @@
         total = total + jnp.sum(block * block, axis=0, keepdims=True)
         toks_t[4 * j : 4 * j + 4] = block.astype(BF16).reshape(4, 32, 128)
     target = (expert_id[...] * 16 + slot_index[...]).astype(F32)
-    aux[0:1, :] = lax.rsqrt(total * (1.0 / 2048.0) + 1e-06)
-    aux[1:2, :] = target
+    aux[0] = lax.rsqrt(total * (1.0 / 2048.0) + 1e-06)
+    aux[1] = target
+    row = gain_in[pl.ds(me // 4, 1), :]
+    turned_gain[...] = jnp.broadcast_to(row, (128, 128)).T
+    chan[0] = turned_gain[pl.ds(pl.multiple_of(me % 4 * 32, 32), 32), :]
+    chan[1] = jnp.broadcast_to(skip_gain[...], (128, 32)).T
     pl.semaphore_wait(barrier, N + 3)
 
     def push(source, dest, sem, device):
@@ -140,30 +148,72 @@
     def held_down(first, count):
         return down.at[pl.ds(512 + down_at + first, count)]
 
-    push(w_up.at[pl.ds(up_at, 512)], held_up(0, 512), 0, {"ctx": across})
-    push(w_down.at[pl.ds(down_at, 64)], held_down(0, 64), 1, {"ctx": across})
-
-    def send_toks(half):
+    def over_x(piece):
+        push(
+            w_up.at[pl.ds(up_at + 256 * piece, 256)], held_up(256 * piece, 256), 2 * piece,
+            {"ctx": across})
+        push(
+            w_down.at[pl.ds(down_at + 32 * piece, 32)], held_down(32 * piece, 32),
+            2 * piece + 1, {"ctx": across})
+
+    def along_grp(piece):
+        settle(held_up(256 * piece, 256), r_w.at[2 * piece])
+        settle(held_down(32 * piece, 32), r_w.at[2 * piece + 1])
+        for first, device in ((0, ahead2), (1, behind2)):
+            some_up = held_up(256 * piece + 128 * first, 128)
+            some_down = held_down(32 * piece + 16 * first, 16)
+            push(some_up, some_up, 4 + 2 * piece, {"grp": device})
+            push(some_down, some_down, 5 + 2 * piece, {"grp": device})
+        for device in (ahead, behind):
+            some_up, some_down = held_up(256 * piece, 256), held_down(32 * piece, 32)
+            push(some_up, some_up, 4 + 2 * piece, {"grp": device})
+            push(some_down, some_down, 5 + 2 * piece, {"grp": device})
+
+    def to_partner(piece):
+        settle(up.at[2, pl.ds(0, 768)], r_w.at[4 + 2 * piece])
+        settle(down.at[pl.ds(512, 96)], r_w.at[5 + 2 * piece])
+        for q in range(4):
+            rows_at = pl.ds(512 * q + 256 * piece, 256)
+            push(up.at[2, rows_at], up.at[3, rows_at], 8, {"ctx": partner})
+            first = 64 * q + 32 * piece
+            push(
+                down.at[pl.ds(512 + first, 32)], down.at[pl.ds(768 + first, 32)], 9,
+                {"ctx": partner})
+
+    over_x(0)
+
+    def send_aux(which, dest, s_sem, r_sem):
+        def send(i, carry):
+            pltpu.make_async_remote_copy(
+                aux.at[which], dest.at[place], s_sem, r_sem,
+                device_id={"ctx": lax.rem(me + i, N)}, device_id_type=MESH).start()
+            return carry
+
+        lax.fori_loop(1, N, send, 0)
+
+    def send_toks(part, carry):
+        channels = pl.ds(pl.multiple_of(WIDE * part, WIDE), WIDE)
+
         def send(i, carry):
             peer = lax.rem(me + i, N)
-            if half == 0:
-                pltpu.make_async_remote_copy(
-                    aux, auxes.at[place], s_aux, r_aux, device_id={"ctx": peer},
-                    device_id_type=MESH).start()
-            channels = pl.ds(16 * half, 16)
             pltpu.make_async_remote_copy(
-                toks_t.at[peer, channels], toks.at[place, channels], s_tok.at[half],
-                r_tok.at[half], device_id={"ctx": peer}, device_id_type=MESH).start()
-            return carry
-
-        lax.fori_loop(1, N, send, 0)
-
-    send_toks(0)
-    send_toks(1)
-    push(w_up, up.at[1], 2, {"ctx": partner})
-    push(w_down, down.at[pl.ds(256, 256)], 3, {"ctx": partner})
+                toks_t.at[peer, channels], toks.at[place, channels], s_tok.at[part],
+                r_tok.at[part], device_id={"ctx": peer}, device_id_type=MESH).start()
+            return carry
+
+        return lax.fori_loop(1, N, send, carry)
+
+    send_aux(0, scales, s_aux, r_aux)
+    lax.fori_loop(0, PARTS, send_toks, 0)
+    over_x(1)
+    send_aux(1, targets, s_tgt, r_tgt)
+    push(w_up, up.at[1], 10, {"ctx": partner})
+    push(w_down, down.at[pl.ds(256, 256)], 11, {"ctx": partner})
     toks[pl.ds(place, 1)] = toks_t[pl.ds(me, 1)]
-    auxes[pl.ds(place, 1)] = aux[...].reshape(1, 2, 128)
+    scales[place] = aux[0]
+    targets[place] = aux[1]
+
+    diag[...] = jnp.zeros_like(diag)
 
     def transform(outer, begin, end):
         def channels(i, carry):
@@ -203,14 +253,7 @@
 
     lax.fori_loop(0, 4, filter_inner, 0)
 
-    settle(held_up(0, 512), r_w.at[0])
-    settle(held_down(0, 64), r_w.at[1])
-    for first, device in ((0, ahead2), (1, behind2)):
-        push(held_up(256 * first, 256), held_up(256 * first, 256), 4, {"grp": device})
-        push(held_down(32 * first, 32), held_down(32 * first, 32), 5, {"grp": device})
-    for device in (ahead, behind):
-        push(held_up(0, 512), held_up(0, 512), 4, {"grp": device})
-        push(held_down(0, 64), held_down(0, 64), 5, {"grp": device})
+    along_grp(0)
 
     def convolve(i, carry):
         at = pl.ds(pl.multiple_of(i * 512, 512), 512)
@@ -229,22 +272,24 @@
                 outer_inv[...], jnp.concatenate([t_h, t_h, t_l], axis=0))
         return carry
 
-    settle(auxes.at[pl.ds(0, N - 1)], r_aux)
-    for half in range(2):
-        begin = 16 * half
-        settle(toks.at[pl.ds(0, N - 1), pl.ds(begin, 16)], r_tok.at[half])
+    settle(scales.at[pl.ds(0, N - 1)], r_aux)
+    for part in range(PARTS):
+        begin = WIDE * part
+        settle(toks.at[pl.ds(0, N - 1), pl.ds(begin, WIDE)], r_tok.at[part])
 
         def load_signal(i, carry):
-            tok = toks[i, begin : begin + 16].astype(F32)
-            normed = (tok * auxes[i, 0:1, :] * chan[0, begin : begin + 16]).astype(BF16)
-            stage[pl.ds(64 * begin + i, 16, stride=64), :] = normed.astype(F32)
+            tok = toks[i, begin : begin + WIDE].astype(F32)
+            normed = (tok * scales[i] * chan[0, begin : begin + WIDE]).astype(BF16)
+            stage[pl.ds(64 * begin + i, WIDE, stride=64), :] = normed.astype(F32)
             return carry
 
         lax.fori_loop(0, N, load_signal, 0)
-        transform(outer_sig, 4 * half, 4 * half + 4)
-        lax.fori_loop(2 * half, 2 * half + 2, convolve, 0)
-
-    diag[...] = jnp.zeros_like(diag)
+        transform(outer_sig, WIDE // 4 * part, WIDE // 4 * (part + 1))
+        lax.fori_loop(WIDE // 8 * part, WIDE // 8 * (part + 1), convolve, 0)
+
+    along_grp(1)
+
+    settle(targets.at[pl.ds(0, N - 1)], r_tgt)
     slot_ids = lax.broadcasted_iota(jnp.int32, (256, 128), 0).astype(F32)
 
     def pack(cls, part):
@@ -252,11 +297,11 @@
         for j in range(4):
             idx = cls * 16 + part * 4 + j
             tok = toks[idx].astype(F32)
-            normed = (tok * auxes[idx, 0:1, :] * chan[0]).astype(BF16).astype(F32)
+            normed = (tok * scales[idx] * chan[0]).astype(BF16).astype(F32)
             conv = stage[pl.ds(idx, 32, stride=64), :]
             conv_out = (conv + chan[1] * normed).astype(BF16).astype(F32)
             diag[32 * j : 32 * j + 32, 128 * j : 128 * j + 128] = (tok + conv_out).astype(BF16)
-            picks.append(jnp.where(slot_ids == auxes[idx, 1:2, :], 1.0, 0.0).astype(BF16))
+            picks.append(jnp.where(slot_ids == targets[idx], 1.0, 0.0).astype(BF16))
         picked = lax.dot_general(
             jnp.concatenate(picks, axis=1), diag[...], (((1,), (1,)), ((), ())),
             preferred_element_type=F32)
@@ -285,13 +330,12 @@
             return carry
 
         lax.fori_loop(0, 4, pack_class, 0)
+        if half == 0:
+            to_partner(0)
 
     rows[pl.ds(me, 1)] = packed[group, pl.ds(expert, 1)]
 
-    settle(up.at[2, pl.ds(0, 1536)], r_w.at[4])
-    settle(down.at[pl.ds(512, 192)], r_w.at[5])
-    push(up.at[2], up.at[3], 6, {"ctx": partner})
-    push(down.at[pl.ds(512, 256)], down.at[pl.ds(768, 256)], 7, {"ctx": partner})
+    to_partner(1)
 
     lane = lax.broadcasted_iota(jnp.int32, (16, 128), 1)
     in_half, in_quarter = lane < 64, lane % 64 < 32
@@ -337,10 +381,10 @@
         if half == 0:
             fetches[2].wait()
             fetches[3].wait()
-            settle(up.at[1], r_w.at[2])
-            settle(down.at[pl.ds(256, 256)], r_w.at[3])
-            settle(up.at[3], r_w.at[6])
-            settle(down.at[pl.ds(768, 256)], r_w.at[7])
+            settle(up.at[1], r_w.at[10])
+            settle(down.at[pl.ds(256, 256)], r_w.at[11])
+            settle(up.at[3], r_w.at[8])
+            settle(down.at[pl.ds(768, 256)], r_w.at[9])
 
         def go_up(i, carry):
             value = dot(ffn_in[these, :], up[i])
@@ -375,21 +419,22 @@
     pick = jnp.where(slot_ids == target, 1.0, 0.0).T.astype(BF16)
     settle(arrived.at[pl.ds(0, 15)], r_out)
 
-    def select(i, carry):
-        at = pl.ds(pl.multiple_of(i * 256, 256), 256)
-        out[:, at] = dot(pick, arrived[:, :, at].reshape(256, 256)).astype(BF16)
-        return carry
-
-    lax.fori_loop(0, 8, select, 0)
-
-    settle(auxes.at[pl.ds(0, N - 1)], s_aux)
+    for i in range(2):
+        at = pl.ds(1024 * i, 1024)
+        out[:, at] = dot(pick, arrived[:, :, at].reshape(256, 1024)).astype(BF16)
+
+    settle(scales.at[pl.ds(0, N - 1)], s_aux)
+    settle(targets.at[pl.ds(0, N - 1)], s_tgt)
+    for part in range(PARTS):
+        settle(toks.at[pl.ds(0, N - 1), pl.ds(WIDE * part, WIDE)], s_tok.at[part])
     for half in range(2):
-        settle(toks.at[pl.ds(0, N - 1), pl.ds(16 * half, 16)], s_tok.at[half])
         settle(rows.at[pl.ds(0, N - 1), pl.ds(32 * half, 32)], s_row.at[half])
     settle(arrived.at[pl.ds(0, 15)], s_out)
     for sem, ref in enumerate((
-        held_up(0, 512), held_down(0, 64), up.at[1], down.at[pl.ds(256, 256)],
-        up.at[2, pl.ds(0, 1536)], down.at[pl.ds(512, 192)], up.at[3], down.at[pl.ds(768, 256)],
+        held_up(0, 256), held_down(0, 32), held_up(256, 256), held_down(32, 32),
+        up.at[2, pl.ds(0, 768)], down.at[pl.ds(512, 96)], up.at[2, pl.ds(0, 768)],
+        down.at[pl.ds(512, 96)], up.at[3], down.at[pl.ds(768, 256)], up.at[1],
+        down.at[pl.ds(256, 256)],
     )):
         settle(ref, s_w.at[sem])
 
@@ -397,9 +442,6 @@
 def body(
     tokens, gain_in, long_filter, skip_gain, gain_ffn, router, w_up, w_down, expert_id, slot_index
 ):
-    me = lax.axis_index("ctx")
-    gain = lax.dynamic_slice(gain_in, (me * 32,), (32,))
-    chan = jnp.broadcast_to(jnp.stack([gain, skip_gain])[:, :, None], (2, 32, 128))
     t = tables()
     consts = [jnp.asarray(t[k]) for k in ("twist", "outer_filt", "outer_sig", "outer_inv", "inner")]
     vmem = pl.BlockSpec(memory_space=pltpu.VMEM)
@@ -408,13 +450,16 @@
     return pl.pallas_call(
         kernel,
         out_shape=jax.ShapeDtypeStruct((128, 2048), BF16),
-        in_specs=[vmem] * 4 + [anywhere] + [vmem] * 2 + [anywhere] * 2 + [vmem] * 4 + [anywhere],
+        in_specs=[vmem] * 5 + [anywhere] + [vmem] * 2 + [anywhere] * 2 + [vmem] * 4 + [anywhere],
         out_specs=vmem,
         scratch_shapes=[
+            pltpu.VMEM((2, 32, 128), F32),
+            pltpu.VMEM((128, 128), F32),
             pltpu.VMEM((N, 32, 128), BF16),
-            pltpu.VMEM((2, 128), F32),
+            pltpu.VMEM((2, 1, 128), F32),
             pltpu.VMEM((N, 32, 128), BF16),
-            pltpu.VMEM((N, 2, 128), F32),
+            pltpu.VMEM((N, 1, 128), F32),
+            pltpu.VMEM((N, 1, 128), F32),
             pltpu.VMEM((32, 8192), BF16),
             pltpu.VMEM((4, 256, 256), BF16),
             pltpu.VMEM((2048, 128), F32),
@@ -431,13 +476,15 @@
             pltpu.VMEM((16, 16, 2048), BF16),
             pltpu.VMEM((4, 2048, 256), BF16),
             pltpu.VMEM((1024, 2048), BF16),
-            dma((2,)), dma((2,)), dma, dma, dma((2,)), dma((2,)), dma, dma, dma((8,)), dma((8,)),
+            dma((PARTS,)), dma((PARTS,)), dma, dma, dma, dma, dma((2,)), dma((2,)), dma, dma, dma((12,)),
+            dma((12,)),
             dma((4,)),
         ],
         compiler_params=pltpu.CompilerParams(
             collective_id=0, has_side_effects=True, vmem_limit_bytes=60 * 1024 * 1024),
     )(
-        tokens, expert_id.reshape(1, 128), slot_index.reshape(1, 128), chan, long_filter,
+        tokens, expert_id.reshape(1, 128), slot_index.reshape(1, 128),
+        gain_in.reshape(16, 128), skip_gain.reshape(1, 32), long_filter,
         gain_ffn.reshape(1, 2048), router.T, w_up, w_down, *consts
     )
 

time: 101 us -> 89.7 us (0.89)
  Pallas kernels: 96.5 us -> 87.7 us
  local copies, waits for them, and re-layouts: 3.92 us -> 1.88 us
    pallas_call x1, Pallas kernels: 96.5 us -> 87.7 us  [body(): pl.pallas_call(kernel, out_shape=jax.ShapeDtypeStruct((128, 2048), BF16),...]
    unnamed x5 -> x1, local copies, waits for them, and re-layouts: 3.16 us -> 1.88 us
where the time goes in v4:
time: 89.7 us; the launch traced here: 89.6 us
  Pallas kernels  87.7 us (98%)
  local copies, waits for them, and re-layouts  1.88 us (2%)
    pallas_call x1, Pallas kernels, body(): pl.pallas_call(kernel, out_shape=jax.ShapeDtypeStruct((128, 2048), BF16),...  87.7 us
    unnamed x1, local copies, waits for them, and re-layouts  1.88 us

profile of v4, /device:TPU:6, one launch (start us, length us, event | category | flops | bytes accessed | tf_op | source)
XLA Modules:
  0.0 89.6 jit_solution(3857912047517738646)
XLA Ops:
  0.0 87.7 %shard_map.145 = bf16[128,2048]{1,0:T(8,128)(2,1)} custom-call(bf16[128,2048]{1,0:T(8,128)(2,1)} %tokens.1, s32[1,128]{1,0:T(1,128)} %bitcast.9, s32[1,128]{1,0:T(1,128)} %bitcast.10, f32[16,128]{1,0:T(8,128)} %bitcast.7, f32[1,32]{1,0:T(1,128)} %bitcast.11, bf16[32,8192]{1,0:T(8,128)(2,1)} %filt_hbm.1, f32[1,2048]{1,0:T(1,128)} %bitcast.8, ...), custom_call_target="tpu_custom_call" | custom-call | tf_op jit(solution)/shard_map/pallas_call | solution.py:450
  87.7 1.9 %copy.17 = bf16[128,2048]{1,0:T(8,128)(2,1)} copy(bf16[128,2048]{1,0:T(8,128)(2,1)} %shard_map.145) | data formatting | bytes 1048576

commit v5 on v4

--- a/solution.py
+++ b/solution.py
@@ -106,7 +106,7 @@
             barrier, inc=1, device_id={"ctx": lax.rem(me + i, N)}, device_id_type=MESH)
         return carry
 
-    lax.fori_loop(1, N, greet, 0)
+    lax.fori_loop(1, N, greet, 0, unroll=7)
     for neighbour in (ahead, behind, ahead2, behind2):
         pl.semaphore_signal(barrier, inc=1, device_id={"grp": neighbour}, device_id_type=MESH)
 
@@ -189,7 +189,7 @@
                 device_id={"ctx": lax.rem(me + i, N)}, device_id_type=MESH).start()
             return carry
 
-        lax.fori_loop(1, N, send, 0)
+        lax.fori_loop(1, N, send, 0, unroll=7)
 
     def send_toks(part, carry):
         channels = pl.ds(pl.multiple_of(WIDE * part, WIDE), WIDE)
@@ -201,7 +201,7 @@
                 r_tok.at[part], device_id={"ctx": peer}, device_id_type=MESH).start()
             return carry
 
-        return lax.fori_loop(1, N, send, carry)
+        return lax.fori_loop(1, N, send, carry, unroll=7)
 
     send_aux(0, scales, s_aux, r_aux)
     lax.fori_loop(0, PARTS, send_toks, 0)
@@ -217,8 +217,8 @@
 
     def transform(outer, begin, end):
         def channels(i, carry):
-            for j in range(4):
-                at = pl.multiple_of((4 * i + j) * 64, 64)
+            for j in range(8):
+                at = pl.multiple_of((8 * i + j) * 64, 64)
                 block = stage[pl.ds(at, 64), :].astype(BF16)
                 first = dot(outer[...], jnp.concatenate([block, block], axis=0))
                 re, im = first[:64], first[64:]
@@ -243,15 +243,15 @@
 
     fetches[0].wait()
     fetches[1].wait()
-    lax.fori_loop(0, N, load_filter, 0)
-    transform(outer_filt, 0, 8)
+    lax.fori_loop(0, N, load_filter, 0, unroll=4)
+    transform(outer_filt, 0, 4)
 
     def filter_inner(i, carry):
         at = pl.ds(pl.multiple_of(i * 512, 512), 512)
         spec[at, :] = inner_dot(high[at, :], low[at, :], 0)
         return carry
 
-    lax.fori_loop(0, 4, filter_inner, 0)
+    lax.fori_loop(0, 4, filter_inner, 0, unroll=2)
 
     along_grp(0)
 
@@ -283,8 +283,8 @@
             stage[pl.ds(64 * begin + i, WIDE, stride=64), :] = normed.astype(F32)
             return carry
 
-        lax.fori_loop(0, N, load_signal, 0)
-        transform(outer_sig, WIDE // 4 * part, WIDE // 4 * (part + 1))
+        lax.fori_loop(0, N, load_signal, 0, unroll=4)
+        transform(outer_sig, WIDE // 8 * part, WIDE // 8 * (part + 1))
         lax.fori_loop(WIDE // 8 * part, WIDE // 8 * (part + 1), convolve, 0)
 
     along_grp(1)
@@ -362,7 +362,7 @@
                     mid[64 * r + 16 * p : 64 * r + 16 * p + 16, at] = u[p]
             return carry
 
-        lax.fori_loop(0, 16, unpack, 0)
+        lax.fori_loop(0, 16, unpack, 0, unroll=2)
 
         def norm_rows(i, carry):
             at = pl.ds(pl.multiple_of(i * 32, 32), 32)
@@ -372,7 +372,7 @@
             ffn_in[at, :] = (block * scale * gain_ffn[...]).astype(BF16)
             return carry
 
-        lax.fori_loop(4 * half, 4 * half + 4, norm_rows, 0)
+        lax.fori_loop(4 * half, 4 * half + 4, norm_rows, 0, unroll=2)
         logits = lax.dot_general(
             ffn_in[these, :], router[...], (((1,), (1,)), ((), ())), preferred_element_type=F32)
         chosen = lax.broadcasted_iota(jnp.int32, logits.shape, 1) == expert
@@ -392,7 +392,7 @@
             hidden[these, pl.ds(pl.multiple_of(i * 256, 256), 256)] = value.astype(BF16)
             return carry
 
-        lax.fori_loop(0, 4, go_up, 0)
+        lax.fori_loop(0, 4, go_up, 0, unroll=2)
 
         def go_down(i, carry):
             at = pl.ds(pl.multiple_of(i * 256, 256), 256)
@@ -401,7 +401,7 @@
             out_rows[8 * half : 8 * half + 8, :, at] = value.reshape(8, 16, 256)
             return carry
 
-        lax.fori_loop(0, 8, go_down, 0)
+        lax.fori_loop(0, 8, go_down, 0, unroll=2)
 
         def send_out(i, carry):
             rank = 8 * half + lax.rem(my_rank + i, 8)

time: 89.7 us -> 87.7 us (0.978)
  Pallas kernels: 87.7 us -> 85.6 us
    pallas_call x1, Pallas kernels: 87.7 us -> 85.6 us  [body(): pl.pallas_call(kernel, out_shape=jax.ShapeDtypeStruct((128, 2048), BF16),...]
where the time goes in v5:
time: 87.7 us; the launch traced here: 87.5 us
  Pallas kernels  85.6 us (98%)
  local copies, waits for them, and re-layouts  1.88 us (2%)
    pallas_call x1, Pallas kernels, body(): pl.pallas_call(kernel, out_shape=jax.ShapeDtypeStruct((128, 2048), BF16),...  85.6 us
    unnamed x1, local copies, waits for them, and re-layouts  1.88 us

profile of v5, /device:TPU:6, one launch (start us, length us, event | category | flops | bytes accessed | tf_op | source)
XLA Modules:
  0.0 87.5 jit_solution(12213138550520780845)
XLA Ops:
  0.0 85.6 %shard_map.145 = bf16[128,2048]{1,0:T(8,128)(2,1)} custom-call(bf16[128,2048]{1,0:T(8,128)(2,1)} %tokens.1, s32[1,128]{1,0:T(1,128)} %bitcast.9, s32[1,128]{1,0:T(1,128)} %bitcast.10, f32[16,128]{1,0:T(8,128)} %bitcast.7, f32[1,32]{1,0:T(1,128)} %bitcast.11, bf16[32,8192]{1,0:T(8,128)(2,1)} %filt_hbm.1, f32[1,2048]{1,0:T(1,128)} %bitcast.8, ...), custom_call_target="tpu_custom_call" | custom-call | tf_op jit(solution)/shard_map/pallas_call | solution.py:450
  85.6 1.9 %copy.17 = bf16[128,2048]{1,0:T(8,128)(2,1)} copy(bf16[128,2048]{1,0:T(8,128)(2,1)} %shard_map.145) | data formatting | bytes 1048576

commit v6 on v5

--- a/solution.py
+++ b/solution.py
@@ -383,8 +383,6 @@
             fetches[3].wait()
             settle(up.at[1], r_w.at[10])
             settle(down.at[pl.ds(256, 256)], r_w.at[11])
-            settle(up.at[3], r_w.at[8])
-            settle(down.at[pl.ds(768, 256)], r_w.at[9])
 
         def go_up(i, carry):
             value = dot(ffn_in[these, :], up[i])
@@ -392,7 +390,12 @@
             hidden[these, pl.ds(pl.multiple_of(i * 256, 256), 256)] = value.astype(BF16)
             return carry
 
-        lax.fori_loop(0, 4, go_up, 0, unroll=2)
+        lax.fori_loop(0, 3, go_up, 0, unroll=3)
+        if half == 0:
+            settle(up.at[3], r_w.at[8])
+        go_up(3, 0)
+        if half == 0:
+            settle(down.at[pl.ds(768, 256)], r_w.at[9])
 
         def go_down(i, carry):
             at = pl.ds(pl.multiple_of(i * 256, 256), 256)

time: 87.7 us -> 87.6 us (level)
  no operation moved by 1% of the time
where the time goes in v6:
time: 87.6 us; the launch traced here: 87.4 us
  Pallas kernels  85.6 us (98%)
  local copies, waits for them, and re-layouts  1.88 us (2%)
    pallas_call x1, Pallas kernels, body(): pl.pallas_call(kernel, out_shape=jax.ShapeDtypeStruct((128, 2048), BF16),...  85.6 us
    unnamed x1, local copies, waits for them, and re-layouts  1.88 us

profile of v6, /device:TPU:6, one launch (start us, length us, event | category | flops | bytes accessed | tf_op | source)
XLA Modules:
  0.0 87.4 jit_solution(16803193015674849473)
XLA Ops:
  0.0 85.6 %shard_map.145 = bf16[128,2048]{1,0:T(8,128)(2,1)} custom-call(bf16[128,2048]{1,0:T(8,128)(2,1)} %tokens.1, s32[1,128]{1,0:T(1,128)} %bitcast.9, s32[1,128]{1,0:T(1,128)} %bitcast.10, f32[16,128]{1,0:T(8,128)} %bitcast.7, f32[1,32]{1,0:T(1,128)} %bitcast.11, bf16[32,8192]{1,0:T(8,128)(2,1)} %filt_hbm.1, f32[1,2048]{1,0:T(1,128)} %bitcast.8, ...), custom_call_target="tpu_custom_call" | custom-call | tf_op jit(solution)/shard_map/pallas_call | solution.py:453
  85.6 1.9 %copy.17 = bf16[128,2048]{1,0:T(8,128)(2,1)} copy(bf16[128,2048]{1,0:T(8,128)(2,1)} %shard_map.145) | data formatting | bytes 1048576

commit v7 on v5

--- a/solution.py
+++ b/solution.py
@@ -15,6 +15,7 @@
 GRP = 8
 PARTS = 2
 WIDE = 32 // PARTS
+FAR_FIRST = (4, 3, 5, 2, 6, 1, 7, 0)
 
 
 def class_of(dev):
@@ -315,8 +316,7 @@
             pack(cls, 2 * half + 1)
             part = pl.ds(32 * half, 32)
 
-            def send(t, carry):
-                to = lax.rem(expert + t, 16)
+            def send(to):
                 dest = holder_of(cls, to)
 
                 @pl.when(dest != me)
@@ -324,9 +324,10 @@
                     pltpu.make_async_remote_copy(
                         packed.at[cls, to, part], rows.at[me, part], s_row.at[half],
                         r_row.at[half], device_id={"ctx": dest}, device_id_type=MESH).start()
-                return carry
-
-            lax.fori_loop(0, 16, send, 0)
+
+            for offset in FAR_FIRST:
+                for pair in range(2):
+                    send(lax.rem(me // 8 + offset, 8) * 2 + pair)
             return carry
 
         lax.fori_loop(0, 4, pack_class, 0)
@@ -403,17 +404,17 @@
 
         lax.fori_loop(0, 8, go_down, 0, unroll=2)
 
-        def send_out(i, carry):
-            rank = 8 * half + lax.rem(my_rank + i, 8)
+        def send_out(offset):
+            rank = 8 * half + lax.rem(my_rank + offset, 8)
 
             @pl.when(rank != my_rank)
             def _():
                 pltpu.make_async_remote_copy(
                     out_rows.at[rank], arrived.at[expert], s_out, r_out,
                     device_id={"ctx": source_of(me, rank)}, device_id_type=MESH).start()
-            return carry
-
-        lax.fori_loop(0, 8, send_out, 0)
+
+        for offset in FAR_FIRST:
+            send_out(offset)
 
     arrived[pl.ds(expert, 1)] = out_rows[pl.ds(my_rank, 1)]
     pick = jnp.where(slot_ids == target, 1.0, 0.0).T.astype(BF16)

time: 87.7 us -> 88.9 us (1.014)
  Pallas kernels: 85.6 us -> 86.9 us
    pallas_call x1, Pallas kernels: 85.6 us -> 86.9 us  [body(): pl.pallas_call(kernel, out_shape=jax.ShapeDtypeStruct((128, 2048), BF16),...]
where the time goes in v7:
time: 88.9 us; the launch traced here: 88.8 us
  Pallas kernels  86.9 us (98%)
  local copies, waits for them, and re-layouts  1.88 us (2%)
    pallas_call x1, Pallas kernels, body(): pl.pallas_call(kernel, out_shape=jax.ShapeDtypeStruct((128, 2048), BF16),...  86.9 us
    unnamed x1, local copies, waits for them, and re-layouts  1.88 us

profile of v7, /device:TPU:6, one launch (start us, length us, event | category | flops | bytes accessed | tf_op | source)
XLA Modules:
  0.0 88.8 jit_solution(14017372317688654997)
XLA Ops:
  0.0 86.9 %shard_map.145 = bf16[128,2048]{1,0:T(8,128)(2,1)} custom-call(bf16[128,2048]{1,0:T(8,128)(2,1)} %tokens.1, s32[1,128]{1,0:T(1,128)} %bitcast.9, s32[1,128]{1,0:T(1,128)} %bitcast.10, f32[16,128]{1,0:T(8,128)} %bitcast.7, f32[1,32]{1,0:T(1,128)} %bitcast.11, bf16[32,8192]{1,0:T(8,128)(2,1)} %filt_hbm.1, f32[1,2048]{1,0:T(1,128)} %bitcast.8, ...), custom_call_target="tpu_custom_call" | custom-call | tf_op jit(solution)/shard_map/pallas_call | solution.py:451
  86.9 1.9 %copy.17 = bf16[128,2048]{1,0:T(8,128)(2,1)} copy(bf16[128,2048]{1,0:T(8,128)(2,1)} %shard_map.145) | data formatting | bytes 1048576
